TPU v7x, 32 devices: a whole 2x2x4 slice. The times are simulated.
32 devices in a mesh: rep: 2 (over x), head: 8 (over z, y), seq: 2 (over core).
Axes of the slice: x: 2, y: 2, z: 4, core: 2. Of those that a mesh axis runs over, the one named last changes fastest.
Arguments:
- q_span: bfloat16 [512, 4096], P(('rep', 'head', 'seq')), parts along dimension 0, may hold values from -6 to 6
- k_span: bfloat16 [512, 1024], P(('rep', 'head', 'seq')), parts along dimension 0, may hold values from -6 to 6
- v_span: bfloat16 [512, 1024], P(('rep', 'head', 'seq')), parts along dimension 0, may hold values from -6 to 6
- k_cache: bfloat16 [16, 8192, 128], P(('rep', 'head'), 'seq'), parts along dimension 0, may hold values from -6 to 6
- v_cache: bfloat16 [16, 8192, 128], P(('rep', 'head'), 'seq'), parts along dimension 0, may hold values from -6 to 6
- head_list: int32 [16], P('rep'), parts along dimension 0, may hold values from 0 to 7, each once
- retrieval: int32 [16], P('rep'), parts along dimension 0, may hold values from 0 to 1
- windows: int32 [16], P('rep'), parts along dimension 0, may hold values from 2049 to 4096
- sinks: int32 [16], P('rep'), parts along dimension 0, may hold values from 1 to 64
Outputs:
- attn_out: bfloat16 [512, 4096], P(('rep', 'head', 'seq')), parts along dimension 0
There are 2 independent parts, one for each index of `rep`. A program takes and returns all parts, laid end to end along the dimension named above; each array names one. Nothing has to cross between parts.
Inputs may be any that keep to these rules, and one draw needn't show every extreme that they name: `head_list`: each kv head stands in exactly one slot.
All inputs are finite; a program needn't handle non-finite values.
Results may differ from a plain program's by a relative error of at most 0.0055.
Values may be sent and summed in bfloat16 or wider, within the bound.
No kernel may reach another device: no remote copies, remote signals or barrier semaphores. Data moves between devices by JAX's collectives and lax.ppermute only.
A program may use at most 64 MiB of HBM per device.

v0:
```python
import functools
import math

import jax
import jax.numpy as jnp
from jax import lax
from jax.experimental import pallas as pl
from jax.experimental.pallas import tpu as pltpu
from jax.sharding import PartitionSpec as P

KVH = 8


NEG_FILL = -1e30


def absorb(
    running,
    query_rows,
    query_pos,
    key_rows,
    value_rows,
    key_pos,
    is_retrieval,
    window_len,
    sink_len,
    score_scale,
):
    top_score, totals, weighted = running
    scores = jnp.dot(query_rows, key_rows.T, preferred_element_type=jnp.float32) * score_scale
    allowed = (key_pos[None, :] <= query_pos[:, None]) & (
        (is_retrieval == 1)
        | (key_pos[None, :] < sink_len)
        | (key_pos[None, :] > query_pos[:, None] - window_len)
    )
    block_top = jnp.max(jnp.where(allowed, scores, NEG_FILL), axis=1)
    new_top = jnp.maximum(top_score, block_top)
    weights = jnp.where(allowed, jnp.exp(scores - new_top[:, None]), 0.0)
    rescale = jnp.exp(top_score - new_top)
    totals = totals * rescale + jnp.sum(weights, axis=1)
    weighted = weighted * rescale[:, None] + jnp.dot(
        weights.astype(jnp.bfloat16), value_rows, preferred_element_type=jnp.float32
    )
    return (new_top, totals, weighted)


def finish_rows(received, spread, head_list, tok_rows, head_dim):
    top_score, totals, weighted = received
    group_heads = top_score.shape[-1]
    top_score = top_score.reshape(KVH, spread, tok_rows, group_heads)
    totals = totals.reshape(KVH, spread, tok_rows, group_heads)
    weighted = weighted.reshape(KVH, spread, tok_rows, group_heads, head_dim)
    overall = jnp.max(top_score, axis=1, keepdims=True)
    factor = jnp.exp(top_score - overall)
    summed = jnp.sum(totals * factor, axis=1)
    combined = jnp.sum(weighted * factor[..., None], axis=1)
    result = combined / summed[..., None]
    matches = (head_list[:, None] == jnp.arange(KVH, dtype=jnp.int32)[None, :]).astype(jnp.int32)
    inverse = jnp.sum(jnp.arange(KVH, dtype=jnp.int32)[:, None] * matches, axis=0)
    by_group = jnp.take(result, inverse, axis=0)
    return (
        by_group.transpose(1, 0, 2, 3)
        .reshape(tok_rows, KVH * group_heads * head_dim)
        .astype(jnp.bfloat16)
    )


def on_device_quarters(q_span, k_span, v_span, k_cache, v_cache, head_list, retrieval, windows, sinks):
    head_count = lax.axis_size("head")
    pair_count = lax.axis_size("seq")
    quarters = head_count // KVH
    tok_rows = q_span.shape[0]
    group_width = q_span.shape[1] // KVH
    head_dim = k_cache.shape[2]
    group_heads = group_width // head_dim
    ctx_dev = k_cache.shape[1]
    total_q = tok_rows * head_count * pair_count
    context = ctx_dev * pair_count * quarters
    head_at = lax.axis_index("head")
    pair_at = lax.axis_index("seq")
    slot_index = head_at // quarters
    quarter = head_at % quarters
    kv_group = jnp.take(head_list, slot_index)
    q_groups = q_span.reshape(tok_rows, KVH, group_width)
    kv_groups = jnp.concatenate(
        [k_span.reshape(tok_rows, KVH, head_dim), v_span.reshape(tok_rows, KVH, head_dim)], axis=2
    )
    targets = jnp.take(head_list, jnp.arange(head_count * pair_count) // pair_count // quarters)
    q_send = jnp.take(q_groups, targets, axis=1)
    kv_send = jnp.take(kv_groups, targets, axis=1)
    q_recv, kv_recv = (
        lax.all_to_all(q_send, ("head", "seq"), split_axis=1, concat_axis=0, tiled=True),
        lax.all_to_all(kv_send, ("head", "seq"), split_axis=1, concat_axis=0, tiled=True),
    )
    queries = q_recv.reshape(total_q, group_width)
    span_kv = kv_recv.reshape(total_q, 2 * head_dim)
    query_rows = queries.reshape(total_q * group_heads, head_dim)
    query_pos = context + jnp.arange(total_q * group_heads, dtype=jnp.int32) // group_heads
    is_retrieval = jnp.take(retrieval, kv_group)
    window_len = jnp.take(windows, kv_group)
    sink_len = jnp.take(sinks, kv_group)
    score_scale = 1.0 / math.sqrt(head_dim)
    row_total = total_q * group_heads
    running = (
        jnp.full((row_total,), NEG_FILL, jnp.float32),
        jnp.zeros((row_total,), jnp.float32),
        jnp.zeros((row_total, head_dim), jnp.float32),
    )
    key_block = min(512, ctx_dev)
    segment = quarter * pair_count + pair_at
    first_key = segment * ctx_dev
    cache_keys = k_cache[0]
    cache_values = v_cache[0]

    def key_step(step_index, state):
        start = step_index * key_block
        key_rows = lax.dynamic_slice_in_dim(cache_keys, start, key_block, 0)
        value_rows = lax.dynamic_slice_in_dim(cache_values, start, key_block, 0)
        key_pos = first_key + start + jnp.arange(key_block, dtype=jnp.int32)
        return absorb(
            state,
            query_rows,
            query_pos,
            key_rows,
            value_rows,
            key_pos,
            is_retrieval,
            window_len,
            sink_len,
            score_scale,
        )

    running = lax.fori_loop(0, ctx_dev // key_block, key_step, running)
    span_piece = total_q // (quarters * pair_count)
    span_start = segment * span_piece
    span_rows = lax.dynamic_slice_in_dim(span_kv, span_start, span_piece, 0)
    span_pos = context + span_start + jnp.arange(span_piece, dtype=jnp.int32)
    top_score, totals, weighted = absorb(
        running,
        query_rows,
        query_pos,
        span_rows[:, :head_dim],
        span_rows[:, head_dim:],
        span_pos,
        is_retrieval,
        window_len,
        sink_len,
        score_scale,
    )
    received = (
        lax.all_to_all(
            top_score.reshape(head_count * pair_count, tok_rows, group_heads),
            ("head", "seq"),
            split_axis=0,
            concat_axis=0,
            tiled=True,
        ),
        lax.all_to_all(
            totals.reshape(head_count * pair_count, tok_rows, group_heads),
            ("head", "seq"),
            split_axis=0,
            concat_axis=0,
            tiled=True,
        ),
        lax.all_to_all(
            weighted.reshape(head_count * pair_count, tok_rows, group_width),
            ("head", "seq"),
            split_axis=0,
            concat_axis=0,
            tiled=True,
        ),
    )
    spread = quarters * pair_count
    return finish_rows(received, spread, head_list, tok_rows, head_dim)


VMEM_SPEC = pl.BlockSpec(memory_space=pltpu.VMEM)
HBM_SPEC = pl.BlockSpec(memory_space=pltpu.HBM)
SMEM_SPEC = pl.BlockSpec(memory_space=pltpu.SMEM)


def pack_kernel(head_ref, in_ref, out_ref, *, group_width, head_dim):
    q_width = KVH * group_width
    q_ref = in_ref.at[:, :q_width]
    k_ref = in_ref.at[:, q_width : q_width + KVH * head_dim]
    v_ref = in_ref.at[:, q_width + KVH * head_dim :]
    for slot in range(out_ref.shape[0]):
        group = head_ref[slot]
        q_start = pl.multiple_of(group * group_width, 128)
        kv_start = pl.multiple_of(group * head_dim, 128)
        out_ref[slot, :, :group_width] = q_ref[:, pl.ds(q_start, group_width)]
        out_ref[slot, :, group_width : group_width + head_dim] = k_ref[:, pl.ds(kv_start, head_dim)]
        out_ref[slot, :, group_width + head_dim :] = v_ref[:, pl.ds(kv_start, head_dim)]


def unpack_kernel(head_ref, in_ref, out_ref, sems):
    width = in_ref.shape[2]
    copies = []
    for slot in range(in_ref.shape[0]):
        start = pl.multiple_of(head_ref[slot] * width, 128)
        copies.append(
            pltpu.make_async_copy(in_ref.at[slot], out_ref.at[:, pl.ds(start, width)], sems.at[slot])
        )
    for copy in copies:
        copy.start()
    for copy in copies:
        copy.wait()


def attend_kernel(
    head_ref,
    retrieval_ref,
    window_ref,
    sink_ref,
    recv_ref,
    peer_ref,
    k_peer,
    v_peer,
    k_source,
    v_source,
    out_ref,
    k_own,
    v_own,
    score_ref,
    top_ref,
    total_ref,
    acc_ref,
    own_sem,
    *,
    tok_rows,
    group_heads,
    head_dim,
    key_block,
    row_block,
):
    k_copy = pltpu.make_async_copy(k_source, k_own, own_sem.at[0])
    v_copy = pltpu.make_async_copy(v_source, v_own, own_sem.at[1])
    k_copy.start()
    pair_at = lax.axis_index("seq")
    kv_group = head_ref[lax.axis_index("head")]
    is_retrieval = retrieval_ref[kv_group]
    window_len = window_ref[kv_group]
    sink_len = sink_ref[kv_group]
    tokens = recv_ref.shape[0]
    rows = tokens * group_heads
    group_width = group_heads * head_dim
    ctx_dev = k_own.shape[0]
    context = 2 * ctx_dev
    f32, bf16 = jnp.float32, jnp.bfloat16
    scale = math.log2(math.e) / math.sqrt(head_dim)

    def token_pos(index, pair):
        return context + ((index // tok_rows) * 2 + pair) * tok_rows + index % tok_rows

    queries = jnp.concatenate(
        [recv_ref[:, k * head_dim : (k + 1) * head_dim] for k in range(group_heads)], axis=0
    )
    scaled = queries.astype(f32) * scale
    high = scaled.astype(bf16)
    low = (scaled - high.astype(f32)).astype(bf16)
    queries = jnp.concatenate([high, low], axis=1)
    row_token = lax.broadcasted_iota(jnp.int32, (1, rows), 1) % tokens
    query_pos = token_pos(row_token, pair_at)

    span_k = pl.ds(group_width, head_dim)
    span_v = pl.ds(group_width + head_dim, head_dim)
    cached, spans = [], []
    for k_ref, v_ref, pair in ((k_peer, v_peer, 1 - pair_at), (k_own, v_own, pair_at)):
        for start in range(0, ctx_dev, key_block):
            cached.append((k_ref, v_ref, start, key_block, pair))
    for ref, pair in ((recv_ref, pair_at), (peer_ref, 1 - pair_at)):
        spans.append((ref, pair))

    def load_keys(index):
        if index < len(cached):
            k_ref, _, start, size, _ = cached[index]
            return k_ref[start : start + size, :]
        return spans[index - len(cached)][0][:, span_k]

    def load_values(index):
        if index < len(cached):
            _, v_ref, start, size, _ = cached[index]
            return v_ref[start : start + size, :]
        return spans[index - len(cached)][0][:, span_v]

    def place(index):
        if index < len(cached):
            return index * key_block, key_block
        return len(cached) * key_block + (index - len(cached)) * tokens, tokens

    def first_pos(index):
        _, _, start, _, pair = cached[index]
        return pair * ctx_dev + start

    def scores(index, row_at, masked):
        keys = load_keys(index)
        keys = jnp.concatenate([keys, keys], axis=1)
        block = lax.dot_general(
            keys,
            queries[row_at : row_at + row_block],
            (((1,), (1,)), ((), ())),
            preferred_element_type=f32,
        )
        size = block.shape[0]
        pos_q = query_pos[:, row_at : row_at + row_block]
        column = lax.broadcasted_iota(jnp.int32, (size, 1), 0)
        allowed = None
        if index >= len(cached):
            pos_k = token_pos(column, spans[index - len(cached)][1])
            allowed = pos_k <= pos_q
        else:
            pos_k = first_pos(index) + column
        if masked:
            near = (pos_k < sink_len) | (pos_k > pos_q - window_len)
            allowed = near if allowed is None else allowed & near
        if allowed is not None:
            block = jnp.where(allowed, block, NEG_FILL)
        start, _ = place(index)
        score_ref[start : start + size, row_at : row_at + row_block] = block
        return jnp.max(block.reshape(size // 8, 8, row_block), axis=0)

    def weighted(index, row_at, top):
        start, size = place(index)
        block = score_ref[start : start + size, row_at : row_at + row_block]
        weights = jnp.exp2(block - top)
        total = jnp.sum(weights.reshape(size // 8, 8, row_block), axis=0)
        acc = lax.dot_general(
            load_values(index),
            weights.astype(bf16),
            (((0,), (0,)), ((), ())),
            preferred_element_type=f32,
        )
        return total, acc

    def finish(row_at, total, acc):
        result = (acc / jnp.sum(total, axis=0, keepdims=True)).T.astype(bf16)
        for start in range(0, row_block, tokens):
            head = (row_at + start) // tokens
            out_ref[:, head * head_dim : (head + 1) * head_dim] = result[start : start + tokens]

    blocks = len(cached) + len(spans)
    row_starts = list(range(0, rows, row_block))

    half = len(cached) // 2
    peer_blocks = list(range(half))
    own_blocks = list(range(half, blocks))

    @pl.when(is_retrieval == 1)
    def _():
        running, total, acc = {}, {}, {}

        def first(indices):
            for row_at in row_starts:
                for index in indices:
                    top = scores(index, row_at, False)
                    running[row_at] = jnp.maximum(running[row_at], top) if row_at in running else top

        def second(indices):
            for row_at in row_starts:
                top = jnp.max(running[row_at], axis=0, keepdims=True)
                for index in indices:
                    part_total, part_acc = weighted(index, row_at, top)
                    total[row_at] = total[row_at] + part_total if row_at in total else part_total
                    acc[row_at] = acc[row_at] + part_acc if row_at in acc else part_acc

        first(peer_blocks)
        k_copy.wait()
        v_copy.start()
        first(own_blocks)
        second(peer_blocks)
        v_copy.wait()
        second(own_blocks)
        for row_at in row_starts:
            finish(row_at, total[row_at], acc[row_at])

    @pl.when(is_retrieval != 1)
    def _():
        def needed(index):
            pos = first_pos(index)
            return (pos < sink_len) | (pos + key_block - 1 > context - window_len)

        top_ref[...] = jnp.full(top_ref.shape, NEG_FILL, f32)
        total_ref[...] = jnp.zeros(total_ref.shape, f32)
        acc_ref[...] = jnp.zeros(acc_ref.shape, f32)

        def first(index):
            for row_at in row_starts:
                cols = slice(row_at, row_at + row_block)
                top_ref[:, cols] = jnp.maximum(top_ref[:, cols], scores(index, row_at, True))

        def second(index):
            for row_at in row_starts:
                cols = slice(row_at, row_at + row_block)
                top = jnp.max(top_ref[:, cols], axis=0, keepdims=True)
                total, acc = weighted(index, row_at, top)
                total_ref[:, cols] += total
                acc_ref[:, cols] += acc

        def each(work, indices):
            for index in indices:
                if index < len(cached):
                    pl.when(needed(index))(functools.partial(work, index))
                else:
                    work(index)

        each(first, peer_blocks)
        k_copy.wait()
        v_copy.start()
        each(first, own_blocks)
        each(second, peer_blocks)
        v_copy.wait()
        each(second, own_blocks)
        for row_at in row_starts:
            cols = slice(row_at, row_at + row_block)
            finish(row_at, total_ref[:, cols], acc_ref[:, cols])


def on_device_pairs(q_span, k_span, v_span, k_cache, v_cache, head_list, retrieval, windows, sinks):
    head_count = lax.axis_size("head")
    tok_rows = q_span.shape[0]
    group_width = q_span.shape[1] // KVH
    head_dim = k_cache.shape[2]
    group_heads = group_width // head_dim
    ctx_dev = k_cache.shape[1]
    tokens = tok_rows * head_count
    rows = tokens * group_heads
    swap = [(0, 1), (1, 0)]
    k_own, v_own = k_cache[0], v_cache[0]
    k_peer = lax.ppermute(k_own, "seq", swap)
    v_peer = lax.ppermute(v_own, "seq", swap)
    joined = jnp.concatenate([q_span, k_span, v_span], axis=1)
    send = pl.pallas_call(
        functools.partial(pack_kernel, group_width=group_width, head_dim=head_dim),
        out_shape=jax.ShapeDtypeStruct((head_count, tok_rows, group_width + 2 * head_dim), jnp.bfloat16),
        in_specs=[SMEM_SPEC, VMEM_SPEC],
        out_specs=VMEM_SPEC,
        compiler_params=pltpu.CompilerParams(vmem_limit_bytes=2**20),
    )(head_list, lax.optimization_barrier(joined))
    recv = lax.all_to_all(send, "head", split_axis=0, concat_axis=0, tiled=True)
    recv = recv.reshape(tokens, group_width + 2 * head_dim)
    peer = lax.ppermute(recv, "seq", swap)
    key_block = math.gcd(ctx_dev, 1024)
    row_block = 256
    keys = 2 * ctx_dev + 2 * tokens
    result = pl.pallas_call(
        functools.partial(
            attend_kernel,
            tok_rows=tok_rows,
            group_heads=group_heads,
            head_dim=head_dim,
            key_block=key_block,
            row_block=row_block,
        ),
        out_shape=jax.ShapeDtypeStruct((tokens, group_width), jnp.bfloat16),
        in_specs=[SMEM_SPEC] * 4 + [VMEM_SPEC] * 4 + [HBM_SPEC] * 2,
        out_specs=VMEM_SPEC,
        scratch_shapes=[
            pltpu.VMEM((ctx_dev, head_dim), jnp.bfloat16),
            pltpu.VMEM((ctx_dev, head_dim), jnp.bfloat16),
            pltpu.VMEM((keys, rows), jnp.float32),
            pltpu.VMEM((8, rows), jnp.float32),
            pltpu.VMEM((8, rows), jnp.float32),
            pltpu.VMEM((head_dim, rows), jnp.float32),
            pltpu.SemaphoreType.DMA((2,)),
        ],
        compiler_params=pltpu.CompilerParams(vmem_limit_bytes=51 * 2**20),
    )(head_list, retrieval, windows, sinks, recv, peer, k_peer, v_peer, k_own, v_own)
    result = result.reshape(head_count, tok_rows, group_width)
    back = lax.all_to_all(result, "head", split_axis=0, concat_axis=0, tiled=True)
    return pl.pallas_call(
        unpack_kernel,
        out_shape=jax.ShapeDtypeStruct((tok_rows, KVH * group_width), jnp.bfloat16),
        in_specs=[SMEM_SPEC, VMEM_SPEC],
        out_specs=HBM_SPEC,
        scratch_shapes=[pltpu.SemaphoreType.DMA((head_count,))],
        compiler_params=pltpu.CompilerParams(vmem_limit_bytes=2**20),
    )(head_list, back)


def solution(mesh):
    on_device = on_device_pairs if mesh.shape["head"] == KVH else on_device_quarters
    in_specs = (
        P(("rep", "head", "seq"), None),
        P(("rep", "head", "seq"), None),
        P(("rep", "head", "seq"), None),
        P(("rep", "head"), "seq", None),
        P(("rep", "head"), "seq", None),
        P("rep"),
        P("rep"),
        P("rep"),
        P("rep"),
    )
    out_specs = P(("rep", "head", "seq"), None)
    return jax.shard_map(
        on_device, mesh=mesh, in_specs=in_specs, out_specs=out_specs, check_vma=False
    )
```

profile of v0, /device:TPU:0, one launch (start us, length us, event | category | flops | bytes accessed | tf_op | source)
XLA Modules:
  0.0 36.1 jit_solution(13489483987077458851)
XLA Ops:
  0.0 0.5 %collective-permute-start.1 = (bf16[4096,128]{1,0:T(8,128)(2,1)}, bf16[4096,128]{1,0:T(8,128)(2,1)S(1)}, u32[]{:S(2)}, u32[]{:S(2)}) collective-permute-start(bf16[4096,128]{1,0:T(8,128)(2,1)} %bitcast.7), channel_id=1, source_target_pairs={{0,1},{1,0},{2,3},{3,2},{4,5},{5,4},{6,7},{7,6},{8,9},{9,8},{10,11... | collective-permute-start | bytes 3145736 | tf_op jit(solution)/shard_map/ppermute | solution.py:429
  0.5 0.0 copy-start
  0.5 0.1 collective-permute-start.2
  0.5 1.0 %pad_maximum_fusion.in_ref = bf16[16,6144]{1,0:T(8,128)(2,1)S(1)} fusion(bf16[16,1024]{1,0:T(8,128)(2,1)} %param.11, bf16[16,1024]{1,0:T(8,128)(2,1)} %param.10, bf16[16,4096]{1,0:T(8,128)(2,1)} %param.9), kind=kLoop, calls=%fused_computation | loop fusion | flops 589824 | bytes 393216 | tf_op jit(solution)/shard_map/concatenate | solution.py:431
  1.5 0.0 copy-done
  1.5 0.6 %shard_map.91 = bf16[8,16,768]{2,1,0:T(8,128)(2,1)S(1)} custom-call(s32[8]{0:T(128)S(1)} %copy-done, bf16[16,6144]{1,0:T(8,128)(2,1)S(1)} %pad_maximum_fusion.in_ref), custom_call_target="tpu_custom_call" | custom-call | tf_op jit(solution)/shard_map/pallas_call | solution.py:432
  2.1 15.3 %all_to_all.10 = bf16[8,16,768]{2,1,0:T(8,128)(2,1)S(1)} all-to-all(bf16[8,16,768]{2,1,0:T(8,128)(2,1)S(1)} %shard_map.91), channel_id=1, replica_groups=mesh['rep'=2,'head'=8,'seq'=2] {'head'}, dimensions={0} | all-to-all | bytes 393216 | tf_op jit(solution)/shard_map/all_to_all | solution.py:439
  17.3 0.0 copy-start.1
  17.3 0.0 copy-start.2
  17.3 0.0 copy-start.3
  17.3 0.0 collective-permute-start
  17.3 1.4 %collective-permute-done.peer_ref = bf16[128,768]{1,0:T(8,128)(2,1)S(1)} collective-permute-done((bf16[128,768]{1,0:T(8,128)(2,1)S(1)}, bf16[128,768]{1,0:T(8,128)(2,1)S(1)}, u32[]{:S(2)}, u32[]{:S(2)}) %collective-permute-start) | collective-permute-done | bytes 196640 | tf_op jit(solution)/shard_map/ppermute | solution.py:441
  18.8 0.0 collective-permute-done.1.k_peer
  18.8 0.0 collective-permute-done.2.v_peer
  18.8 0.0 copy-done.1
  18.8 0.0 copy-done.2
  18.8 0.0 copy-done.3
  18.8 5.2 %shard_map.92 = bf16[128,512]{1,0:T(8,128)(2,1)S(1)} custom-call(s32[8]{0:T(128)S(1)} %copy-done, s32[8]{0:T(128)S(1)} %copy-done.1, s32[8]{0:T(128)S(1)} %copy-done.2, s32[8]{0:T(128)S(1)} %copy-done.3, bf16[128,768]{1,0:T(8,128)(2,1)S(1)} %bitcast.5, bf16[128,768]{1,0:T(8,128)(2,1)S(1)} %collective-permute-done.peer_ref, ...), custom_call_target="tpu_custom_call" | custom-call | tf_op jit(solution)/shard_map/pallas_call | solution.py:445
  24.1 10.8 %all_to_all.11.in_ref = bf16[8,16,512]{2,1,0:T(8,128)(2,1)S(1)} all-to-all(bf16[8,16,512]{2,1,0:T(8,128)(2,1)S(1)} %bitcast.6), channel_id=1, replica_groups=mesh['rep'=2,'head'=8,'seq'=2] {'head'}, dimensions={0} | all-to-all | bytes 262144 | tf_op jit(solution)/shard_map/all_to_all | solution.py:469
  34.9 1.3 %shard_map.93 = bf16[16,4096]{1,0:T(8,128)(2,1)} custom-call(s32[8]{0:T(128)S(1)} %copy-done, bf16[8,16,512]{2,1,0:T(8,128)(2,1)S(1)} %all_to_all.11.in_ref), custom_call_target="tpu_custom_call" | custom-call | tf_op jit(solution)/shard_map/pallas_call | solution.py:470
Async XLA Ops:
  0.0 18.8 %collective-permute-start.1 = (bf16[4096,128]{1,0:T(8,128)(2,1)}, bf16[4096,128]{1,0:T(8,128)(2,1)S(1)}, u32[]{:S(2)}, u32[]{:S(2)}) collective-permute-start(bf16[4096,128]{1,0:T(8,128)(2,1)} %bitcast.7), channel_id=1, source_target_pairs={{0,1},{1,0},{2,3},{3,2},{4,5},{5,4},{6,7},{7,6},{8,9},{9,8},{10,11... | collective-permute-start | bytes 3145736 | tf_op jit(solution)/shard_map/ppermute | solution.py:429
  0.5 1.0 %copy-start = (s32[8]{0:T(128)S(1)}, s32[8]{0:T(128)}, u32[]{:S(2)}) copy-start(s32[8]{0:T(128)} %head_ref.5) | copy-start | bytes 100
  0.5 18.3 %collective-permute-start.2 = (bf16[4096,128]{1,0:T(8,128)(2,1)}, bf16[4096,128]{1,0:T(8,128)(2,1)S(1)}, u32[]{:S(2)}, u32[]{:S(2)}) collective-permute-start(bf16[4096,128]{1,0:T(8,128)(2,1)} %bitcast.9), channel_id=1, source_target_pairs={{0,1},{1,0},{2,3},{3,2},{4,5},{5,4},{6,7},{7,6},{8,9},{9,8},{10,11... | collective-permute-start | bytes 3145736 | tf_op jit(solution)/shard_map/ppermute | solution.py:430
  17.3 1.5 %copy-start.1 = (s32[8]{0:T(128)S(1)}, s32[8]{0:T(128)}, u32[]{:S(2)}) copy-start(s32[8]{0:T(128)} %retrieval_ref.1) | copy-start | bytes 100
  17.3 1.5 %copy-start.2 = (s32[8]{0:T(128)S(1)}, s32[8]{0:T(128)}, u32[]{:S(2)}) copy-start(s32[8]{0:T(128)} %window_ref.1) | copy-start | bytes 100
  17.3 1.5 %copy-start.3 = (s32[8]{0:T(128)S(1)}, s32[8]{0:T(128)}, u32[]{:S(2)}) copy-start(s32[8]{0:T(128)} %sink_ref.1) | copy-start | bytes 100
  17.3 1.4 %collective-permute-start = (bf16[128,768]{1,0:T(8,128)(2,1)S(1)}, bf16[128,768]{1,0:T(8,128)(2,1)S(1)}, u32[]{:S(2)}, u32[]{:S(2)}) collective-permute-start(bf16[128,768]{1,0:T(8,128)(2,1)S(1)} %bitcast.4), channel_id=1, source_target_pairs={{0,1},{1,0},{2,3},{3,2},{4,5},{5,4},{6,7},{7,6},{8,9},{9,8},{10,11... | collective-permute-start | bytes 589832 | tf_op jit(solution)/shard_map/ppermute | solution.py:441
where the time goes:
time: 36.4 us; the launch traced here: 36.1 us
  blocking collectives  26.1 us (72%)
  Pallas kernels  7.07 us (19%)
  waiting for transfers between devices  1.44 us (4%)
  other arithmetic  0.96 us (3%)
  starting transfers between devices  0.52 us (1%)
    all_to_all x1, blocking collectives, on_device_pairs(): recv = lax.all_to_all(send, 'head', split_axis=0, concat_axis=0, tiled=True)  15.3 us
    all_to_all x1, blocking collectives, on_device_pairs(): lax.all_to_all(result, 'head', split_axis=0, concat_axis=0, tiled=True)  10.8 us
    pallas_call x1, Pallas kernels, on_device_pairs(): pl.pallas_call(functools.partial(attend_kernel, tok_rows=tok_rows, group_...  5.24 us
    ppermute x1, waiting for transfers between devices, on_device_pairs(): peer = lax.ppermute(recv, 'seq', swap)  1.43 us
    pallas_call x1, Pallas kernels, on_device_pairs(): pl.pallas_call(unpack_kernel, out_shape=jax.ShapeDtypeStruct((tok_rows, K...  1.26 us
    concatenate x1, other arithmetic, on_device_pairs(): joined = jnp.concatenate([q_span, k_span, v_span], axis=1)  0.96 us
  transfers between devices with their start and end apart: 3, of which 1 were waited for; matrix products, arithmetic and copies ran while one was open for 3% of the time, Pallas kernels for 2%

commit v1 on v0

--- a/solution.py
+++ b/solution.py
@@ -207,24 +207,88 @@
         copy.wait()
 
 
+def stack_queries(recv_ref, group_heads, head_dim):
+    scale = math.log2(math.e) / math.sqrt(head_dim)
+    queries = jnp.concatenate(
+        [recv_ref[:, k * head_dim : (k + 1) * head_dim] for k in range(group_heads)], axis=0
+    )
+    scaled = queries.astype(jnp.float32) * scale
+    high = scaled.astype(jnp.bfloat16)
+    low = (scaled - high.astype(jnp.float32)).astype(jnp.bfloat16)
+    return jnp.concatenate([high, low], axis=1)
+
+
+def span_kernel(
+    head_ref,
+    retrieval_ref,
+    window_ref,
+    sink_ref,
+    recv_ref,
+    peer_ref,
+    acc_ref,
+    stat_ref,
+    out_ref,
+    *,
+    tok_rows,
+    group_heads,
+    head_dim,
+    context,
+):
+    f32, bf16 = jnp.float32, jnp.bfloat16
+    pair_at = lax.axis_index("seq")
+    kv_group = head_ref[lax.axis_index("head")]
+    is_retrieval = retrieval_ref[kv_group]
+    window_len = jnp.where(is_retrieval == 1, 2**30, window_ref[kv_group])
+    sink_len = sink_ref[kv_group]
+    tokens = recv_ref.shape[0]
+    rows = tokens * group_heads
+    group_width = group_heads * head_dim
+    queries = stack_queries(recv_ref, group_heads, head_dim)
+
+    def token_pos(index, pair):
+        return context + ((index // tok_rows) * 2 + pair) * tok_rows + index % tok_rows
+
+    query_pos = token_pos(lax.broadcasted_iota(jnp.int32, (1, rows), 1) % tokens, pair_at)
+    key_pos = token_pos(lax.broadcasted_iota(jnp.int32, (tokens, 1), 0), 1 - pair_at)
+    keys = peer_ref[:, group_width : group_width + head_dim]
+    values = peer_ref[:, group_width + head_dim : group_width + 2 * head_dim]
+    block = lax.dot_general(
+        jnp.concatenate([keys, keys], axis=1),
+        queries,
+        (((1,), (1,)), ((), ())),
+        preferred_element_type=f32,
+    )
+    allowed = (key_pos <= query_pos) & ((key_pos < sink_len) | (key_pos > query_pos - window_len))
+    block = jnp.where(allowed, block, NEG_FILL)
+    old_top = stat_ref[0:1, :]
+    top = jnp.maximum(old_top, jnp.max(block, axis=0, keepdims=True))
+    factor = jnp.exp2(old_top - top)
+    weights = jnp.exp2(block - top)
+    total = jnp.sum(stat_ref[8:16, :], axis=0, keepdims=True) * factor
+    total = total + jnp.sum(weights, axis=0, keepdims=True)
+    acc = acc_ref[...] * factor + lax.dot_general(
+        values, weights.astype(bf16), (((0,), (0,)), ((), ())), preferred_element_type=f32
+    )
+    result = (acc / total).T.astype(bf16)
+    for head in range(group_heads):
+        out_ref[:, head * head_dim : (head + 1) * head_dim] = result[head * tokens : (head + 1) * tokens]
+
+
 def attend_kernel(
     head_ref,
     retrieval_ref,
     window_ref,
     sink_ref,
     recv_ref,
-    peer_ref,
     k_peer,
     v_peer,
     k_source,
     v_source,
-    out_ref,
+    acc_ref,
+    stat_ref,
     k_own,
     v_own,
     score_ref,
-    top_ref,
-    total_ref,
-    acc_ref,
     own_sem,
     *,
     tok_rows,
@@ -247,18 +311,10 @@
     ctx_dev = k_own.shape[0]
     context = 2 * ctx_dev
     f32, bf16 = jnp.float32, jnp.bfloat16
-    scale = math.log2(math.e) / math.sqrt(head_dim)
-
     def token_pos(index, pair):
         return context + ((index // tok_rows) * 2 + pair) * tok_rows + index % tok_rows
 
-    queries = jnp.concatenate(
-        [recv_ref[:, k * head_dim : (k + 1) * head_dim] for k in range(group_heads)], axis=0
-    )
-    scaled = queries.astype(f32) * scale
-    high = scaled.astype(bf16)
-    low = (scaled - high.astype(f32)).astype(bf16)
-    queries = jnp.concatenate([high, low], axis=1)
+    queries = stack_queries(recv_ref, group_heads, head_dim)
     row_token = lax.broadcasted_iota(jnp.int32, (1, rows), 1) % tokens
     query_pos = token_pos(row_token, pair_at)
 
@@ -268,8 +324,7 @@
     for k_ref, v_ref, pair in ((k_peer, v_peer, 1 - pair_at), (k_own, v_own, pair_at)):
         for start in range(0, ctx_dev, key_block):
             cached.append((k_ref, v_ref, start, key_block, pair))
-    for ref, pair in ((recv_ref, pair_at), (peer_ref, 1 - pair_at)):
-        spans.append((ref, pair))
+    spans.append((recv_ref, pair_at))
 
     def load_keys(index):
         if index < len(cached):
@@ -332,12 +387,6 @@
         )
         return total, acc
 
-    def finish(row_at, total, acc):
-        result = (acc / jnp.sum(total, axis=0, keepdims=True)).T.astype(bf16)
-        for start in range(0, row_block, tokens):
-            head = (row_at + start) // tokens
-            out_ref[:, head * head_dim : (head + 1) * head_dim] = result[start : start + tokens]
-
     blocks = len(cached) + len(spans)
     row_starts = list(range(0, rows, row_block))
 
@@ -371,7 +420,11 @@
         v_copy.wait()
         second(own_blocks)
         for row_at in row_starts:
-            finish(row_at, total[row_at], acc[row_at])
+            cols = slice(row_at, row_at + row_block)
+            top = jnp.max(running[row_at], axis=0, keepdims=True)
+            stat_ref[0:8, cols] = jnp.broadcast_to(top, (8, row_block))
+            stat_ref[8:16, cols] = total[row_at]
+            acc_ref[:, cols] = acc[row_at]
 
     @pl.when(is_retrieval != 1)
     def _():
@@ -379,21 +432,21 @@
             pos = first_pos(index)
             return (pos < sink_len) | (pos + key_block - 1 > context - window_len)
 
-        top_ref[...] = jnp.full(top_ref.shape, NEG_FILL, f32)
-        total_ref[...] = jnp.zeros(total_ref.shape, f32)
+        stat_ref[0:8, :] = jnp.full((8, rows), NEG_FILL, f32)
+        stat_ref[8:16, :] = jnp.zeros((8, rows), f32)
         acc_ref[...] = jnp.zeros(acc_ref.shape, f32)
 
         def first(index):
             for row_at in row_starts:
                 cols = slice(row_at, row_at + row_block)
-                top_ref[:, cols] = jnp.maximum(top_ref[:, cols], scores(index, row_at, True))
+                stat_ref[0:8, cols] = jnp.maximum(stat_ref[0:8, cols], scores(index, row_at, True))
 
         def second(index):
             for row_at in row_starts:
                 cols = slice(row_at, row_at + row_block)
-                top = jnp.max(top_ref[:, cols], axis=0, keepdims=True)
+                top = jnp.max(stat_ref[0:8, cols], axis=0, keepdims=True)
                 total, acc = weighted(index, row_at, top)
-                total_ref[:, cols] += total
+                stat_ref[8:16, cols] += total
                 acc_ref[:, cols] += acc
 
         def each(work, indices):
@@ -410,9 +463,8 @@
         each(second, peer_blocks)
         v_copy.wait()
         each(second, own_blocks)
-        for row_at in row_starts:
-            cols = slice(row_at, row_at + row_block)
-            finish(row_at, total_ref[:, cols], acc_ref[:, cols])
+        top = jnp.max(stat_ref[0:8, :], axis=0, keepdims=True)
+        stat_ref[0:8, :] = jnp.broadcast_to(top, (8, rows))
 
 
 def on_device_pairs(q_span, k_span, v_span, k_cache, v_cache, head_list, retrieval, windows, sinks):
@@ -441,8 +493,8 @@
     peer = lax.ppermute(recv, "seq", swap)
     key_block = math.gcd(ctx_dev, 1024)
     row_block = 256
-    keys = 2 * ctx_dev + 2 * tokens
-    result = pl.pallas_call(
+    keys = 2 * ctx_dev + tokens
+    acc, stat = pl.pallas_call(
         functools.partial(
             attend_kernel,
             tok_rows=tok_rows,
@@ -451,20 +503,33 @@
             key_block=key_block,
             row_block=row_block,
         ),
-        out_shape=jax.ShapeDtypeStruct((tokens, group_width), jnp.bfloat16),
-        in_specs=[SMEM_SPEC] * 4 + [VMEM_SPEC] * 4 + [HBM_SPEC] * 2,
-        out_specs=VMEM_SPEC,
+        out_shape=(
+            jax.ShapeDtypeStruct((head_dim, rows), jnp.float32),
+            jax.ShapeDtypeStruct((16, rows), jnp.float32),
+        ),
+        in_specs=[SMEM_SPEC] * 4 + [VMEM_SPEC] * 3 + [HBM_SPEC] * 2,
+        out_specs=(VMEM_SPEC, VMEM_SPEC),
         scratch_shapes=[
             pltpu.VMEM((ctx_dev, head_dim), jnp.bfloat16),
             pltpu.VMEM((ctx_dev, head_dim), jnp.bfloat16),
             pltpu.VMEM((keys, rows), jnp.float32),
-            pltpu.VMEM((8, rows), jnp.float32),
-            pltpu.VMEM((8, rows), jnp.float32),
-            pltpu.VMEM((head_dim, rows), jnp.float32),
             pltpu.SemaphoreType.DMA((2,)),
         ],
         compiler_params=pltpu.CompilerParams(vmem_limit_bytes=51 * 2**20),
-    )(head_list, retrieval, windows, sinks, recv, peer, k_peer, v_peer, k_own, v_own)
+    )(head_list, retrieval, windows, sinks, recv, k_peer, v_peer, k_own, v_own)
+    result = pl.pallas_call(
+        functools.partial(
+            span_kernel,
+            tok_rows=tok_rows,
+            group_heads=group_heads,
+            head_dim=head_dim,
+            context=2 * ctx_dev,
+        ),
+        out_shape=jax.ShapeDtypeStruct((tokens, group_width), jnp.bfloat16),
+        in_specs=[SMEM_SPEC] * 4 + [VMEM_SPEC] * 4,
+        out_specs=VMEM_SPEC,
+        compiler_params=pltpu.CompilerParams(vmem_limit_bytes=4 * 2**20),
+    )(head_list, retrieval, windows, sinks, recv, peer, acc, stat)
     result = result.reshape(head_count, tok_rows, group_width)
     back = lax.all_to_all(result, "head", split_axis=0, concat_axis=0, tiled=True)
     return pl.pallas_call(

time: 36.4 us -> 36.6 us (level)
  Pallas kernels: 7.07 us -> 8.55 us
  waiting for transfers between devices: 1.44 us -> 0.01 us
  blocking collectives: 26.1 us -> 25.3 us
  local copies, waits for them, and re-layouts: 0.01 us -> 0.66 us
    ppermute x1, waiting for transfers between devices: 1.43 us -> 0.01 us  [on_device_pairs(): peer = lax.ppermute(recv, 'seq', swap)]
    pallas_call x0 -> x1, Pallas kernels: none -> 1.09 us  [on_device_pairs(): pl.pallas_call(functools.partial(span_kernel, tok_rows=tok_rows, group_he...]
    all_to_all x1, blocking collectives: 10.8 us -> 10 us  [on_device_pairs(): lax.all_to_all(result, 'head', split_axis=0, concat_axis=0, tiled=True)]
    unnamed x8, local copies, waits for them, and re-layouts: 0.01 us -> 0.66 us
    pallas_call x1, Pallas kernels: 5.24 us -> 5.63 us  [on_device_pairs(): pl.pallas_call(functools.partial(attend_kernel, tok_rows=tok_rows, group_...]
  transfers between devices with their start and end apart: 3 -> 3, of which waited for: 1 -> 0; matrix products, arithmetic and copies ran while one was open for 3% -> 3% of each run, Pallas kernels for 2% -> 17%
where the time goes in v1:
time: 36.6 us; the launch traced here: 36 us
  blocking collectives  25.3 us (69%)
  Pallas kernels  8.55 us (23%)
  other arithmetic  0.96 us (3%)
  local copies, waits for them, and re-layouts  0.66 us (2%)
  starting transfers between devices  0.52 us (1%)
    all_to_all x1, blocking collectives, on_device_pairs(): recv = lax.all_to_all(send, 'head', split_axis=0, concat_axis=0, tiled=True)  15.3 us
    all_to_all x1, blocking collectives, on_device_pairs(): lax.all_to_all(result, 'head', split_axis=0, concat_axis=0, tiled=True)  10 us
    pallas_call x1, Pallas kernels, on_device_pairs(): pl.pallas_call(functools.partial(attend_kernel, tok_rows=tok_rows, group_...  5.63 us
    pallas_call x1, Pallas kernels, on_device_pairs(): pl.pallas_call(unpack_kernel, out_shape=jax.ShapeDtypeStruct((tok_rows, K...  1.26 us
    pallas_call x1, Pallas kernels, on_device_pairs(): pl.pallas_call(functools.partial(span_kernel, tok_rows=tok_rows, group_he...  1.09 us
    concatenate x1, other arithmetic, on_device_pairs(): joined = jnp.concatenate([q_span, k_span, v_span], axis=1)  0.96 us
  transfers between devices with their start and end apart: 3, of which 0 were waited for; matrix products, arithmetic and copies ran while one was open for 3% of the time, Pallas kernels for 17%

profile of v1, /device:TPU:0, one launch (start us, length us, event | category | flops | bytes accessed | tf_op | source)
XLA Modules:
  0.0 36.0 jit_solution(921124268614028084)
XLA Ops:
  0.0 0.5 %collective-permute-start.1 = (bf16[4096,128]{1,0:T(8,128)(2,1)}, bf16[4096,128]{1,0:T(8,128)(2,1)S(1)}, u32[]{:S(2)}, u32[]{:S(2)}) collective-permute-start(bf16[4096,128]{1,0:T(8,128)(2,1)} %bitcast.8), channel_id=1, source_target_pairs={{0,1},{1,0},{2,3},{3,2},{4,5},{5,4},{6,7},{7,6},{8,9},{9,8},{10,11... | collective-permute-start | bytes 3145736 | tf_op jit(solution)/shard_map/ppermute | solution.py:481
  0.5 0.0 copy-start
  0.5 0.1 collective-permute-start.2
  0.5 1.0 %pad_maximum_fusion.in_ref = bf16[16,6144]{1,0:T(8,128)(2,1)S(1)} fusion(bf16[16,1024]{1,0:T(8,128)(2,1)} %param.11, bf16[16,1024]{1,0:T(8,128)(2,1)} %param.10, bf16[16,4096]{1,0:T(8,128)(2,1)} %param.9), kind=kLoop, calls=%fused_computation | loop fusion | flops 589824 | bytes 393216 | tf_op jit(solution)/shard_map/concatenate | solution.py:483
  1.5 0.0 copy-done
  1.5 0.6 %shard_map.91 = bf16[8,16,768]{2,1,0:T(8,128)(2,1)S(1)} custom-call(s32[8]{0:T(128)S(1)} %copy-done, bf16[16,6144]{1,0:T(8,128)(2,1)S(1)} %pad_maximum_fusion.in_ref), custom_call_target="tpu_custom_call" | custom-call | tf_op jit(solution)/shard_map/pallas_call | solution.py:484
  2.1 15.3 %all_to_all.10 = bf16[8,16,768]{2,1,0:T(8,128)(2,1)S(1)} all-to-all(bf16[8,16,768]{2,1,0:T(8,128)(2,1)S(1)} %shard_map.91), channel_id=1, replica_groups=mesh['rep'=2,'head'=8,'seq'=2] {'head'}, dimensions={0} | all-to-all | bytes 393216 | tf_op jit(solution)/shard_map/all_to_all | solution.py:491
  17.3 0.0 copy-start.1
  17.3 0.0 copy-start.2
  17.3 0.0 copy-start.3
  17.3 0.0 collective-permute-start
  17.3 0.0 collective-permute-done.1.k_peer
  17.4 0.0 collective-permute-done.2.v_peer
  17.4 0.6 %copy-done.1 = s32[8]{0:T(128)S(1)} copy-done((s32[8]{0:T(128)S(1)}, s32[8]{0:T(128)}, u32[]{:S(2)}) %copy-start.1) | copy-done | bytes 56
  18.0 0.0 copy-done.2
  18.0 0.0 copy-done.3
  18.0 5.6 %shard_map.92 = (f32[128,512]{1,0:T(8,128)S(1)}, f32[16,512]{1,0:T(8,128)S(1)}) custom-call(s32[8]{0:T(128)S(1)} %copy-done, s32[8]{0:T(128)S(1)} %copy-done.1, s32[8]{0:T(128)S(1)} %copy-done.2, s32[8]{0:T(128)S(1)} %copy-done.3, bf16[128,768]{1,0:T(8,128)(2,1)S(1)} %bitcast.5, bf16[4096,128]{1,0:T(8,128)(2,1)S(1)} %collective-permute-done.1.k_peer, ...), custom_call_target="tpu_custom_call" | custom-call | tf_op jit(solution)/shard_map/pallas_call | solution.py:497
  23.6 0.0 collective-permute-done.peer_ref
  23.7 1.1 %shard_map.93 = bf16[128,512]{1,0:T(8,128)(2,1)S(1)} custom-call(s32[8]{0:T(128)S(1)} %copy-done, s32[8]{0:T(128)S(1)} %copy-done.1, s32[8]{0:T(128)S(1)} %copy-done.2, s32[8]{0:T(128)S(1)} %copy-done.3, bf16[128,768]{1,0:T(8,128)(2,1)S(1)} %bitcast.6, bf16[128,768]{1,0:T(8,128)(2,1)S(1)} %collective-permute-done.peer_ref, ...), custom_call_target="tpu_custom_call" | custom-call | tf_op jit(solution)/shard_map/pallas_call | solution.py:520
  24.8 10.0 %all_to_all.11.in_ref = bf16[8,16,512]{2,1,0:T(8,128)(2,1)S(1)} all-to-all(bf16[8,16,512]{2,1,0:T(8,128)(2,1)S(1)} %bitcast.7), channel_id=1, replica_groups=mesh['rep'=2,'head'=8,'seq'=2] {'head'}, dimensions={0} | all-to-all | bytes 262144 | tf_op jit(solution)/shard_map/all_to_all | solution.py:534
  34.8 1.3 %shard_map.94 = bf16[16,4096]{1,0:T(8,128)(2,1)} custom-call(s32[8]{0:T(128)S(1)} %copy-done, bf16[8,16,512]{2,1,0:T(8,128)(2,1)S(1)} %all_to_all.11.in_ref), custom_call_target="tpu_custom_call" | custom-call | tf_op jit(solution)/shard_map/pallas_call | solution.py:535
Async XLA Ops:
  0.0 17.3 %collective-permute-start.1 = (bf16[4096,128]{1,0:T(8,128)(2,1)}, bf16[4096,128]{1,0:T(8,128)(2,1)S(1)}, u32[]{:S(2)}, u32[]{:S(2)}) collective-permute-start(bf16[4096,128]{1,0:T(8,128)(2,1)} %bitcast.8), channel_id=1, source_target_pairs={{0,1},{1,0},{2,3},{3,2},{4,5},{5,4},{6,7},{7,6},{8,9},{9,8},{10,11... | collective-permute-start | bytes 3145736 | tf_op jit(solution)/shard_map/ppermute | solution.py:481
  0.5 1.0 %copy-start = (s32[8]{0:T(128)S(1)}, s32[8]{0:T(128)}, u32[]{:S(2)}) copy-start(s32[8]{0:T(128)} %head_ref.7) | copy-start | bytes 100
  0.5 16.9 %collective-permute-start.2 = (bf16[4096,128]{1,0:T(8,128)(2,1)}, bf16[4096,128]{1,0:T(8,128)(2,1)S(1)}, u32[]{:S(2)}, u32[]{:S(2)}) collective-permute-start(bf16[4096,128]{1,0:T(8,128)(2,1)} %bitcast.10), channel_id=1, source_target_pairs={{0,1},{1,0},{2,3},{3,2},{4,5},{5,4},{6,7},{7,6},{8,9},{9,8},{10,11... | collective-permute-start | bytes 3145736 | tf_op jit(solution)/shard_map/ppermute | solution.py:482
  17.3 0.7 %copy-start.1 = (s32[8]{0:T(128)S(1)}, s32[8]{0:T(128)}, u32[]{:S(2)}) copy-start(s32[8]{0:T(128)} %retrieval_ref.3) | copy-start | bytes 100
  17.3 0.7 %copy-start.2 = (s32[8]{0:T(128)S(1)}, s32[8]{0:T(128)}, u32[]{:S(2)}) copy-start(s32[8]{0:T(128)} %window_ref.3) | copy-start | bytes 100
  17.3 0.7 %copy-start.3 = (s32[8]{0:T(128)S(1)}, s32[8]{0:T(128)}, u32[]{:S(2)}) copy-start(s32[8]{0:T(128)} %sink_ref.3) | copy-start | bytes 100
  17.3 6.3 %collective-permute-start = (bf16[128,768]{1,0:T(8,128)(2,1)S(1)}, bf16[128,768]{1,0:T(8,128)(2,1)S(1)}, u32[]{:S(2)}, u32[]{:S(2)}) collective-permute-start(bf16[128,768]{1,0:T(8,128)(2,1)S(1)} %bitcast.4), channel_id=1, source_target_pairs={{0,1},{1,0},{2,3},{3,2},{4,5},{5,4},{6,7},{7,6},{8,9},{9,8},{10,11... | collective-permute-start | bytes 589832 | tf_op jit(solution)/shard_map/ppermute | solution.py:493

commit v2 on v1

--- a/solution.py
+++ b/solution.py
@@ -179,7 +179,13 @@
 SMEM_SPEC = pl.BlockSpec(memory_space=pltpu.SMEM)
 
 
-def pack_kernel(head_ref, in_ref, out_ref, *, group_width, head_dim):
+def pack_kernel(
+    head_ref, retrieval_ref, window_ref, sink_ref, in_ref, out_ref, info_ref, *, group_width, head_dim
+):
+    kv_group = head_ref[lax.axis_index("head")]
+    info_ref[0] = retrieval_ref[kv_group]
+    info_ref[1] = window_ref[kv_group]
+    info_ref[2] = sink_ref[kv_group]
     q_width = KVH * group_width
     q_ref = in_ref.at[:, :q_width]
     k_ref = in_ref.at[:, q_width : q_width + KVH * head_dim]
@@ -219,10 +225,7 @@
 
 
 def span_kernel(
-    head_ref,
-    retrieval_ref,
-    window_ref,
-    sink_ref,
+    info_ref,
     recv_ref,
     peer_ref,
     acc_ref,
@@ -236,10 +239,8 @@
 ):
     f32, bf16 = jnp.float32, jnp.bfloat16
     pair_at = lax.axis_index("seq")
-    kv_group = head_ref[lax.axis_index("head")]
-    is_retrieval = retrieval_ref[kv_group]
-    window_len = jnp.where(is_retrieval == 1, 2**30, window_ref[kv_group])
-    sink_len = sink_ref[kv_group]
+    window_len = jnp.where(info_ref[0] == 1, 2**30, info_ref[1])
+    sink_len = info_ref[2]
     tokens = recv_ref.shape[0]
     rows = tokens * group_heads
     group_width = group_heads * head_dim
@@ -275,10 +276,7 @@
 
 
 def attend_kernel(
-    head_ref,
-    retrieval_ref,
-    window_ref,
-    sink_ref,
+    info_ref,
     recv_ref,
     k_peer,
     v_peer,
@@ -301,10 +299,7 @@
     v_copy = pltpu.make_async_copy(v_source, v_own, own_sem.at[1])
     k_copy.start()
     pair_at = lax.axis_index("seq")
-    kv_group = head_ref[lax.axis_index("head")]
-    is_retrieval = retrieval_ref[kv_group]
-    window_len = window_ref[kv_group]
-    sink_len = sink_ref[kv_group]
+    is_retrieval, window_len, sink_len = (info_ref[i] for i in range(3))
     tokens = recv_ref.shape[0]
     rows = tokens * group_heads
     group_width = group_heads * head_dim
@@ -481,13 +476,16 @@
     k_peer = lax.ppermute(k_own, "seq", swap)
     v_peer = lax.ppermute(v_own, "seq", swap)
     joined = jnp.concatenate([q_span, k_span, v_span], axis=1)
-    send = pl.pallas_call(
+    send, info = pl.pallas_call(
         functools.partial(pack_kernel, group_width=group_width, head_dim=head_dim),
-        out_shape=jax.ShapeDtypeStruct((head_count, tok_rows, group_width + 2 * head_dim), jnp.bfloat16),
-        in_specs=[SMEM_SPEC, VMEM_SPEC],
-        out_specs=VMEM_SPEC,
+        out_shape=(
+            jax.ShapeDtypeStruct((head_count, tok_rows, group_width + 2 * head_dim), jnp.bfloat16),
+            jax.ShapeDtypeStruct((3,), jnp.int32),
+        ),
+        in_specs=[SMEM_SPEC] * 4 + [VMEM_SPEC],
+        out_specs=(VMEM_SPEC, SMEM_SPEC),
         compiler_params=pltpu.CompilerParams(vmem_limit_bytes=2**20),
-    )(head_list, lax.optimization_barrier(joined))
+    )(head_list, retrieval, windows, sinks, lax.optimization_barrier(joined))
     recv = lax.all_to_all(send, "head", split_axis=0, concat_axis=0, tiled=True)
     recv = recv.reshape(tokens, group_width + 2 * head_dim)
     peer = lax.ppermute(recv, "seq", swap)
@@ -507,7 +505,7 @@
             jax.ShapeDtypeStruct((head_dim, rows), jnp.float32),
             jax.ShapeDtypeStruct((16, rows), jnp.float32),
         ),
-        in_specs=[SMEM_SPEC] * 4 + [VMEM_SPEC] * 3 + [HBM_SPEC] * 2,
+        in_specs=[SMEM_SPEC] + [VMEM_SPEC] * 3 + [HBM_SPEC] * 2,
         out_specs=(VMEM_SPEC, VMEM_SPEC),
         scratch_shapes=[
             pltpu.VMEM((ctx_dev, head_dim), jnp.bfloat16),
@@ -516,7 +514,7 @@
             pltpu.SemaphoreType.DMA((2,)),
         ],
         compiler_params=pltpu.CompilerParams(vmem_limit_bytes=51 * 2**20),
-    )(head_list, retrieval, windows, sinks, recv, k_peer, v_peer, k_own, v_own)
+    )(info, recv, k_peer, v_peer, k_own, v_own)
     result = pl.pallas_call(
         functools.partial(
             span_kernel,
@@ -526,10 +524,10 @@
             context=2 * ctx_dev,
         ),
         out_shape=jax.ShapeDtypeStruct((tokens, group_width), jnp.bfloat16),
-        in_specs=[SMEM_SPEC] * 4 + [VMEM_SPEC] * 4,
+        in_specs=[SMEM_SPEC] + [VMEM_SPEC] * 4,
         out_specs=VMEM_SPEC,
         compiler_params=pltpu.CompilerParams(vmem_limit_bytes=4 * 2**20),
-    )(head_list, retrieval, windows, sinks, recv, peer, acc, stat)
+    )(info, recv, peer, acc, stat)
     result = result.reshape(head_count, tok_rows, group_width)
     back = lax.all_to_all(result, "head", split_axis=0, concat_axis=0, tiled=True)
     return pl.pallas_call(

time: 36.6 us -> 37.8 us (1.033)
  blocking collectives: 25.3 us -> 26.4 us
  Pallas kernels: 8.55 us -> 9.54 us
  local copies, waits for them, and re-layouts: 0.66 us -> 0.01 us
    all_to_all x1, blocking collectives: 10 us -> 11.2 us  [on_device_pairs(): lax.all_to_all(result, 'head', split_axis=0, concat_axis=0, tiled=True)]
    unnamed x8, local copies, waits for them, and re-layouts: 0.66 us -> 0.01 us
    pallas_call x1, Pallas kernels: 0.58 us -> 1.19 us  [on_device_pairs(): pl.pallas_call(functools.partial(pack_kernel, group_width=group_width, he...]
    pallas_call x1, Pallas kernels: 5.63 us -> 6.03 us  [on_device_pairs(): pl.pallas_call(functools.partial(attend_kernel, tok_rows=tok_rows, group_...]
  transfers between devices with their start and end apart: 3 -> 3, of which waited for: 0 -> 0; matrix products, arithmetic and copies ran while one was open for 3% -> 3% of each run, Pallas kernels for 17% -> 19%
where the time goes in v2:
time: 37.8 us; the launch traced here: 37.6 us
  blocking collectives  26.4 us (70%)
  Pallas kernels  9.54 us (25%)
  other arithmetic  0.96 us (3%)
  starting transfers between devices  0.58 us (2%)
    all_to_all x1, blocking collectives, on_device_pairs(): recv = lax.all_to_all(send, 'head', split_axis=0, concat_axis=0, tiled=True)  15.2 us
    all_to_all x1, blocking collectives, on_device_pairs(): lax.all_to_all(result, 'head', split_axis=0, concat_axis=0, tiled=True)  11.2 us
    pallas_call x1, Pallas kernels, on_device_pairs(): pl.pallas_call(functools.partial(attend_kernel, tok_rows=tok_rows, group_...  6.03 us
    pallas_call x1, Pallas kernels, on_device_pairs(): pl.pallas_call(unpack_kernel, out_shape=jax.ShapeDtypeStruct((tok_rows, K...  1.26 us
    pallas_call x1, Pallas kernels, on_device_pairs(): pl.pallas_call(functools.partial(pack_kernel, group_width=group_width, he...  1.19 us
    pallas_call x1, Pallas kernels, on_device_pairs(): pl.pallas_call(functools.partial(span_kernel, tok_rows=tok_rows, group_he...  1.07 us
    concatenate x1, other arithmetic, on_device_pairs(): joined = jnp.concatenate([q_span, k_span, v_span], axis=1)  0.96 us
  transfers between devices with their start and end apart: 3, of which 0 were waited for; matrix products, arithmetic and copies ran while one was open for 3% of the time, Pallas kernels for 19%

profile of v2, /device:TPU:0, one launch (start us, length us, event | category | flops | bytes accessed | tf_op | source)
XLA Modules:
  0.0 37.6 jit_solution(14967425207438598857)
XLA Ops:
  0.0 0.5 %collective-permute-start.1 = (bf16[4096,128]{1,0:T(8,128)(2,1)}, bf16[4096,128]{1,0:T(8,128)(2,1)S(1)}, u32[]{:S(2)}, u32[]{:S(2)}) collective-permute-start(bf16[4096,128]{1,0:T(8,128)(2,1)} %bitcast.8), channel_id=1, source_target_pairs={{0,1},{1,0},{2,3},{3,2},{4,5},{5,4},{6,7},{7,6},{8,9},{9,8},{10,11... | collective-permute-start | bytes 3145736 | tf_op jit(solution)/shard_map/ppermute | solution.py:476
  0.5 0.0 copy-start
  0.5 0.0 copy-start.1
  0.5 0.0 copy-start.2
  0.5 0.0 copy-start.3
  0.5 0.1 collective-permute-start.2
  0.6 1.0 %pad_maximum_fusion.in_ref = bf16[16,6144]{1,0:T(8,128)(2,1)S(1)} fusion(bf16[16,1024]{1,0:T(8,128)(2,1)} %param.11, bf16[16,1024]{1,0:T(8,128)(2,1)} %param.10, bf16[16,4096]{1,0:T(8,128)(2,1)} %param.9), kind=kLoop, calls=%fused_computation | loop fusion | flops 589824 | bytes 393216 | tf_op jit(solution)/shard_map/concatenate | solution.py:478
  1.5 0.0 copy-done
  1.6 0.0 copy-done.1
  1.6 0.0 copy-done.2
  1.6 0.0 copy-done.3
  1.6 1.2 %shard_map.91 = (bf16[8,16,768]{2,1,0:T(8,128)(2,1)S(1)}, s32[3]{0:T(128)S(1)}) custom-call(s32[8]{0:T(128)S(1)} %copy-done, s32[8]{0:T(128)S(1)} %copy-done.1, s32[8]{0:T(128)S(1)} %copy-done.2, s32[8]{0:T(128)S(1)} %copy-done.3, bf16[16,6144]{1,0:T(8,128)(2,1)S(1)} %pad_maximum_fusion.in_ref), custom_call_target="tpu_custom_call" | custom-call | tf_op jit(solution)/shard_map/pallas_call | solution.py:479
  2.8 15.2 %all_to_all.10 = bf16[8,16,768]{2,1,0:T(8,128)(2,1)S(1)} all-to-all(bf16[8,16,768]{2,1,0:T(8,128)(2,1)S(1)} %get-tuple-element.10), channel_id=1, replica_groups=mesh['rep'=2,'head'=8,'seq'=2] {'head'}, dimensions={0} | all-to-all | bytes 393216 | tf_op jit(solution)/shard_map/all_to_all | solution.py:489
  18.0 0.0 collective-permute-start
  18.0 0.0 collective-permute-done.1.k_peer
  18.0 0.0 collective-permute-done.2.v_peer
  18.0 6.0 %shard_map.92 = (f32[128,512]{1,0:T(8,128)S(1)}, f32[16,512]{1,0:T(8,128)S(1)}) custom-call(s32[3]{0:T(128)S(1)} %get-tuple-element.9.info_ref, bf16[128,768]{1,0:T(8,128)(2,1)S(1)} %bitcast.5, bf16[4096,128]{1,0:T(8,128)(2,1)S(1)} %collective-permute-done.1.k_peer, bf16[4096,128]{1,0:T(8,128)(2,1)S(1)} %collective-permute-done.2.v_peer, ...), custom_call_target="tpu_custom_call" | custom-call | tf_op jit(solution)/shard_map/pallas_call | solution.py:495
  24.1 0.0 collective-permute-done.peer_ref
  24.1 1.1 %shard_map.93 = bf16[128,512]{1,0:T(8,128)(2,1)S(1)} custom-call(s32[3]{0:T(128)S(1)} %get-tuple-element.9.info_ref, bf16[128,768]{1,0:T(8,128)(2,1)S(1)} %bitcast.6, bf16[128,768]{1,0:T(8,128)(2,1)S(1)} %collective-permute-done.peer_ref, f32[128,512]{1,0:T(8,128)S(1)} %get-tuple-element.11.acc_ref, f32[16,512]{1,0:T(8,128)S(1)} %get-tuple-element.12.stat_ref), custom_call_target="tpu_custom_call" | custom-call | tf_op jit(solution)/shard_map/pallas_call | solution.py:518
  25.1 11.2 %all_to_all.11.in_ref = bf16[8,16,512]{2,1,0:T(8,128)(2,1)S(1)} all-to-all(bf16[8,16,512]{2,1,0:T(8,128)(2,1)S(1)} %bitcast.7), channel_id=1, replica_groups=mesh['rep'=2,'head'=8,'seq'=2] {'head'}, dimensions={0} | all-to-all | bytes 262144 | tf_op jit(solution)/shard_map/all_to_all | solution.py:532
  36.3 1.3 %shard_map.94 = bf16[16,4096]{1,0:T(8,128)(2,1)} custom-call(s32[8]{0:T(128)S(1)} %copy-done, bf16[8,16,512]{2,1,0:T(8,128)(2,1)S(1)} %all_to_all.11.in_ref), custom_call_target="tpu_custom_call" | custom-call | tf_op jit(solution)/shard_map/pallas_call | solution.py:533
Async XLA Ops:
  0.0 18.0 %collective-permute-start.1 = (bf16[4096,128]{1,0:T(8,128)(2,1)}, bf16[4096,128]{1,0:T(8,128)(2,1)S(1)}, u32[]{:S(2)}, u32[]{:S(2)}) collective-permute-start(bf16[4096,128]{1,0:T(8,128)(2,1)} %bitcast.8), channel_id=1, source_target_pairs={{0,1},{1,0},{2,3},{3,2},{4,5},{5,4},{6,7},{7,6},{8,9},{9,8},{10,11... | collective-permute-start | bytes 3145736 | tf_op jit(solution)/shard_map/ppermute | solution.py:476
  0.5 1.1 %copy-start = (s32[8]{0:T(128)S(1)}, s32[8]{0:T(128)}, u32[]{:S(2)}) copy-start(s32[8]{0:T(128)} %head_ref.3) | copy-start | bytes 100
  0.5 1.1 %copy-start.1 = (s32[8]{0:T(128)S(1)}, s32[8]{0:T(128)}, u32[]{:S(2)}) copy-start(s32[8]{0:T(128)} %retrieval_ref.1) | copy-start | bytes 100
  0.5 1.1 %copy-start.2 = (s32[8]{0:T(128)S(1)}, s32[8]{0:T(128)}, u32[]{:S(2)}) copy-start(s32[8]{0:T(128)} %window_ref.1) | copy-start | bytes 100
  0.5 1.1 %copy-start.3 = (s32[8]{0:T(128)S(1)}, s32[8]{0:T(128)}, u32[]{:S(2)}) copy-start(s32[8]{0:T(128)} %sink_ref.1) | copy-start | bytes 100
  0.5 17.5 %collective-permute-start.2 = (bf16[4096,128]{1,0:T(8,128)(2,1)}, bf16[4096,128]{1,0:T(8,128)(2,1)S(1)}, u32[]{:S(2)}, u32[]{:S(2)}) collective-permute-start(bf16[4096,128]{1,0:T(8,128)(2,1)} %bitcast.10), channel_id=1, source_target_pairs={{0,1},{1,0},{2,3},{3,2},{4,5},{5,4},{6,7},{7,6},{8,9},{9,8},{10,11... | collective-permute-start | bytes 3145736 | tf_op jit(solution)/shard_map/ppermute | solution.py:477
  18.0 6.0 %collective-permute-start = (bf16[128,768]{1,0:T(8,128)(2,1)S(1)}, bf16[128,768]{1,0:T(8,128)(2,1)S(1)}, u32[]{:S(2)}, u32[]{:S(2)}) collective-permute-start(bf16[128,768]{1,0:T(8,128)(2,1)S(1)} %bitcast.4), channel_id=1, source_target_pairs={{0,1},{1,0},{2,3},{3,2},{4,5},{5,4},{6,7},{7,6},{8,9},{9,8},{10,11... | collective-permute-start | bytes 589832 | tf_op jit(solution)/shard_map/ppermute | solution.py:491

commit v3 on v1

--- a/solution.py
+++ b/solution.py
@@ -207,6 +207,11 @@
         copy.wait()
 
 
+def look_up(table_ref):
+    kv_group = table_ref[lax.axis_index("head")]
+    return (table_ref[part * KVH + kv_group] for part in (1, 2, 3))
+
+
 def stack_queries(recv_ref, group_heads, head_dim):
     scale = math.log2(math.e) / math.sqrt(head_dim)
     queries = jnp.concatenate(
@@ -219,10 +224,7 @@
 
 
 def span_kernel(
-    head_ref,
-    retrieval_ref,
-    window_ref,
-    sink_ref,
+    table_ref,
     recv_ref,
     peer_ref,
     acc_ref,
@@ -236,10 +238,8 @@
 ):
     f32, bf16 = jnp.float32, jnp.bfloat16
     pair_at = lax.axis_index("seq")
-    kv_group = head_ref[lax.axis_index("head")]
-    is_retrieval = retrieval_ref[kv_group]
-    window_len = jnp.where(is_retrieval == 1, 2**30, window_ref[kv_group])
-    sink_len = sink_ref[kv_group]
+    is_retrieval, window_len, sink_len = look_up(table_ref)
+    window_len = jnp.where(is_retrieval == 1, 2**30, window_len)
     tokens = recv_ref.shape[0]
     rows = tokens * group_heads
     group_width = group_heads * head_dim
@@ -275,10 +275,7 @@
 
 
 def attend_kernel(
-    head_ref,
-    retrieval_ref,
-    window_ref,
-    sink_ref,
+    table_ref,
     recv_ref,
     k_peer,
     v_peer,
@@ -301,10 +298,7 @@
     v_copy = pltpu.make_async_copy(v_source, v_own, own_sem.at[1])
     k_copy.start()
     pair_at = lax.axis_index("seq")
-    kv_group = head_ref[lax.axis_index("head")]
-    is_retrieval = retrieval_ref[kv_group]
-    window_len = window_ref[kv_group]
-    sink_len = sink_ref[kv_group]
+    is_retrieval, window_len, sink_len = look_up(table_ref)
     tokens = recv_ref.shape[0]
     rows = tokens * group_heads
     group_width = group_heads * head_dim
@@ -481,13 +475,15 @@
     k_peer = lax.ppermute(k_own, "seq", swap)
     v_peer = lax.ppermute(v_own, "seq", swap)
     joined = jnp.concatenate([q_span, k_span, v_span], axis=1)
+    joined, *indices = lax.optimization_barrier((joined, head_list, retrieval, windows, sinks))
+    table = jnp.concatenate(indices)
     send = pl.pallas_call(
         functools.partial(pack_kernel, group_width=group_width, head_dim=head_dim),
         out_shape=jax.ShapeDtypeStruct((head_count, tok_rows, group_width + 2 * head_dim), jnp.bfloat16),
         in_specs=[SMEM_SPEC, VMEM_SPEC],
         out_specs=VMEM_SPEC,
         compiler_params=pltpu.CompilerParams(vmem_limit_bytes=2**20),
-    )(head_list, lax.optimization_barrier(joined))
+    )(table, joined)
     recv = lax.all_to_all(send, "head", split_axis=0, concat_axis=0, tiled=True)
     recv = recv.reshape(tokens, group_width + 2 * head_dim)
     peer = lax.ppermute(recv, "seq", swap)
@@ -507,7 +503,7 @@
             jax.ShapeDtypeStruct((head_dim, rows), jnp.float32),
             jax.ShapeDtypeStruct((16, rows), jnp.float32),
         ),
-        in_specs=[SMEM_SPEC] * 4 + [VMEM_SPEC] * 3 + [HBM_SPEC] * 2,
+        in_specs=[SMEM_SPEC] + [VMEM_SPEC] * 3 + [HBM_SPEC] * 2,
         out_specs=(VMEM_SPEC, VMEM_SPEC),
         scratch_shapes=[
             pltpu.VMEM((ctx_dev, head_dim), jnp.bfloat16),
@@ -516,7 +512,7 @@
             pltpu.SemaphoreType.DMA((2,)),
         ],
         compiler_params=pltpu.CompilerParams(vmem_limit_bytes=51 * 2**20),
-    )(head_list, retrieval, windows, sinks, recv, k_peer, v_peer, k_own, v_own)
+    )(table, recv, k_peer, v_peer, k_own, v_own)
     result = pl.pallas_call(
         functools.partial(
             span_kernel,
@@ -526,10 +522,10 @@
             context=2 * ctx_dev,
         ),
         out_shape=jax.ShapeDtypeStruct((tokens, group_width), jnp.bfloat16),
-        in_specs=[SMEM_SPEC] * 4 + [VMEM_SPEC] * 4,
+        in_specs=[SMEM_SPEC] + [VMEM_SPEC] * 4,
         out_specs=VMEM_SPEC,
         compiler_params=pltpu.CompilerParams(vmem_limit_bytes=4 * 2**20),
-    )(head_list, retrieval, windows, sinks, recv, peer, acc, stat)
+    )(table, recv, peer, acc, stat)
     result = result.reshape(head_count, tok_rows, group_width)
     back = lax.all_to_all(result, "head", split_axis=0, concat_axis=0, tiled=True)
     return pl.pallas_call(
@@ -539,7 +535,7 @@
         out_specs=HBM_SPEC,
         scratch_shapes=[pltpu.SemaphoreType.DMA((head_count,))],
         compiler_params=pltpu.CompilerParams(vmem_limit_bytes=2**20),
-    )(head_list, back)
+    )(table, back)
 
 
 def solution(mesh):

time: 36.6 us -> 36.2 us (0.989); the launches traced: 36 us -> 36.1 us
  local copies, waits for them, and re-layouts: 0.66 us -> 0.01 us
  blocking collectives: 25.3 us -> 25.8 us
    unnamed x8, local copies, waits for them, and re-layouts: 0.66 us -> 0.01 us
    all_to_all x1, blocking collectives: 10 us -> 10.6 us  [on_device_pairs(): lax.all_to_all(result, 'head', split_axis=0, concat_axis=0, tiled=True)]
where the time goes in v3:
time: 36.2 us; the launch traced here: 36.1 us
  blocking collectives  25.8 us (71%)
  Pallas kernels  8.58 us (24%)
  other arithmetic  1.04 us (3%)
  starting transfers between devices  0.58 us (2%)
    all_to_all x1, blocking collectives, on_device_pairs(): recv = lax.all_to_all(send, 'head', split_axis=0, concat_axis=0, tiled=True)  15.2 us
    all_to_all x1, blocking collectives, on_device_pairs(): lax.all_to_all(result, 'head', split_axis=0, concat_axis=0, tiled=True)  10.6 us
    pallas_call x1, Pallas kernels, on_device_pairs(): pl.pallas_call(functools.partial(attend_kernel, tok_rows=tok_rows, group_...  5.68 us
    pallas_call x1, Pallas kernels, on_device_pairs(): pl.pallas_call(unpack_kernel, out_shape=jax.ShapeDtypeStruct((tok_rows, K...  1.26 us
    pallas_call x1, Pallas kernels, on_device_pairs(): pl.pallas_call(functools.partial(span_kernel, tok_rows=tok_rows, group_he...  1.07 us
    concatenate x1, other arithmetic, on_device_pairs(): joined = jnp.concatenate([q_span, k_span, v_span], axis=1)  0.96 us
  transfers between devices with their start and end apart: 3, of which 0 were waited for; matrix products, arithmetic and copies ran while one was open for 3% of the time, Pallas kernels for 17%

profile of v3, /device:TPU:0, one launch (start us, length us, event | category | flops | bytes accessed | tf_op | source)
XLA Modules:
  0.0 36.1 jit_solution(11617153075776615120)
XLA Ops:
  0.0 0.5 %collective-permute-start.1 = (bf16[4096,128]{1,0:T(8,128)(2,1)}, bf16[4096,128]{1,0:T(8,128)(2,1)S(1)}, u32[]{:S(2)}, u32[]{:S(2)}) collective-permute-start(bf16[4096,128]{1,0:T(8,128)(2,1)} %bitcast.8), channel_id=1, source_target_pairs={{0,1},{1,0},{2,3},{3,2},{4,5},{5,4},{6,7},{7,6},{8,9},{9,8},{10,11... | collective-permute-start | bytes 3145736 | tf_op jit(solution)/shard_map/ppermute | solution.py:475
  0.5 0.0 copy-start
  0.5 0.0 copy-start.1
  0.5 0.0 copy-start.2
  0.5 0.0 copy-start.3
  0.5 0.1 collective-permute-start.2
  0.6 1.0 %pad_maximum_fusion.in_ref = bf16[16,6144]{1,0:T(8,128)(2,1)S(1)} fusion(bf16[16,1024]{1,0:T(8,128)(2,1)} %param.11, bf16[16,1024]{1,0:T(8,128)(2,1)} %param.10, bf16[16,4096]{1,0:T(8,128)(2,1)} %param.9), kind=kLoop, calls=%fused_computation | loop fusion | flops 589824 | bytes 393216 | tf_op jit(solution)/shard_map/concatenate | solution.py:477
  1.5 0.0 copy-done
  1.6 0.0 copy-done.1
  1.6 0.0 copy-done.2
  1.6 0.0 copy-done.3
  1.6 0.1 pad_add_fusion.head_ref.table_ref
  1.7 0.6 %shard_map.91 = bf16[8,16,768]{2,1,0:T(8,128)(2,1)S(1)} custom-call(s32[32]{0:T(128)S(1)} %pad_add_fusion.head_ref.table_ref, bf16[16,6144]{1,0:T(8,128)(2,1)S(1)} %pad_maximum_fusion.in_ref), custom_call_target="tpu_custom_call" | custom-call | tf_op jit(solution)/shard_map/pallas_call | solution.py:480
  2.2 15.2 %all_to_all.10 = bf16[8,16,768]{2,1,0:T(8,128)(2,1)S(1)} all-to-all(bf16[8,16,768]{2,1,0:T(8,128)(2,1)S(1)} %shard_map.91), channel_id=1, replica_groups=mesh['rep'=2,'head'=8,'seq'=2] {'head'}, dimensions={0} | all-to-all | bytes 393216 | tf_op jit(solution)/shard_map/all_to_all | solution.py:487
  17.5 0.0 collective-permute-start
  17.5 0.0 collective-permute-done.1.k_peer
  17.5 0.0 collective-permute-done.2.v_peer
  17.5 5.7 %shard_map.92 = (f32[128,512]{1,0:T(8,128)S(1)}, f32[16,512]{1,0:T(8,128)S(1)}) custom-call(s32[32]{0:T(128)S(1)} %pad_add_fusion.head_ref.table_ref, bf16[128,768]{1,0:T(8,128)(2,1)S(1)} %bitcast.5, bf16[4096,128]{1,0:T(8,128)(2,1)S(1)} %collective-permute-done.1.k_peer, bf16[4096,128]{1,0:T(8,128)(2,1)S(1)} %collective-permute-done.2.v_peer, ...), custom_call_target="tpu_custom_call" | custom-call | tf_op jit(solution)/shard_map/pallas_call | solution.py:493
  23.2 0.0 collective-permute-done.peer_ref
  23.2 1.1 %shard_map.93 = bf16[128,512]{1,0:T(8,128)(2,1)S(1)} custom-call(s32[32]{0:T(128)S(1)} %pad_add_fusion.head_ref.table_ref, bf16[128,768]{1,0:T(8,128)(2,1)S(1)} %bitcast.6, bf16[128,768]{1,0:T(8,128)(2,1)S(1)} %collective-permute-done.peer_ref, f32[128,512]{1,0:T(8,128)S(1)} %get-tuple-element.17.acc_ref, f32[16,512]{1,0:T(8,128)S(1)} %get-tuple-element.18.stat_ref), custom_call_target="tpu_custom_call" | custom-call | tf_op jit(solution)/shard_map/pallas_call | solution.py:516
  24.3 10.6 %all_to_all.11.in_ref = bf16[8,16,512]{2,1,0:T(8,128)(2,1)S(1)} all-to-all(bf16[8,16,512]{2,1,0:T(8,128)(2,1)S(1)} %bitcast.7), channel_id=1, replica_groups=mesh['rep'=2,'head'=8,'seq'=2] {'head'}, dimensions={0} | all-to-all | bytes 262144 | tf_op jit(solution)/shard_map/all_to_all | solution.py:530
  34.8 1.3 %shard_map.94 = bf16[16,4096]{1,0:T(8,128)(2,1)} custom-call(s32[32]{0:T(128)S(1)} %pad_add_fusion.head_ref.table_ref, bf16[8,16,512]{2,1,0:T(8,128)(2,1)S(1)} %all_to_all.11.in_ref), custom_call_target="tpu_custom_call" | custom-call | tf_op jit(solution)/shard_map/pallas_call | solution.py:531
Async XLA Ops:
  0.0 17.5 %collective-permute-start.1 = (bf16[4096,128]{1,0:T(8,128)(2,1)}, bf16[4096,128]{1,0:T(8,128)(2,1)S(1)}, u32[]{:S(2)}, u32[]{:S(2)}) collective-permute-start(bf16[4096,128]{1,0:T(8,128)(2,1)} %bitcast.8), channel_id=1, source_target_pairs={{0,1},{1,0},{2,3},{3,2},{4,5},{5,4},{6,7},{7,6},{8,9},{9,8},{10,11... | collective-permute-start | bytes 3145736 | tf_op jit(solution)/shard_map/ppermute | solution.py:475
  0.5 1.1 %copy-start = (s32[8]{0:T(128)S(1)}, s32[8]{0:T(128)}, u32[]{:S(2)}) copy-start(s32[8]{0:T(128)} %param.17) | copy-start | bytes 100
  0.5 1.1 %copy-start.1 = (s32[8]{0:T(128)S(1)}, s32[8]{0:T(128)}, u32[]{:S(2)}) copy-start(s32[8]{0:T(128)} %param.16) | copy-start | bytes 100
  0.5 1.1 %copy-start.2 = (s32[8]{0:T(128)S(1)}, s32[8]{0:T(128)}, u32[]{:S(2)}) copy-start(s32[8]{0:T(128)} %param.15) | copy-start | bytes 100
  0.5 1.1 %copy-start.3 = (s32[8]{0:T(128)S(1)}, s32[8]{0:T(128)}, u32[]{:S(2)}) copy-start(s32[8]{0:T(128)} %param.14) | copy-start | bytes 100
  0.5 17.0 %collective-permute-start.2 = (bf16[4096,128]{1,0:T(8,128)(2,1)}, bf16[4096,128]{1,0:T(8,128)(2,1)S(1)}, u32[]{:S(2)}, u32[]{:S(2)}) collective-permute-start(bf16[4096,128]{1,0:T(8,128)(2,1)} %bitcast.10), channel_id=1, source_target_pairs={{0,1},{1,0},{2,3},{3,2},{4,5},{5,4},{6,7},{7,6},{8,9},{9,8},{10,11... | collective-permute-start | bytes 3145736 | tf_op jit(solution)/shard_map/ppermute | solution.py:476
  17.5 5.7 %collective-permute-start = (bf16[128,768]{1,0:T(8,128)(2,1)S(1)}, bf16[128,768]{1,0:T(8,128)(2,1)S(1)}, u32[]{:S(2)}, u32[]{:S(2)}) collective-permute-start(bf16[128,768]{1,0:T(8,128)(2,1)S(1)} %bitcast.4), channel_id=1, source_target_pairs={{0,1},{1,0},{2,3},{3,2},{4,5},{5,4},{6,7},{7,6},{8,9},{9,8},{10,11... | collective-permute-start | bytes 589832 | tf_op jit(solution)/shard_map/ppermute | solution.py:489

commit v4 on v3

--- a/solution.py
+++ b/solution.py
@@ -294,9 +294,33 @@
     key_block,
     row_block,
 ):
-    k_copy = pltpu.make_async_copy(k_source, k_own, own_sem.at[0])
-    v_copy = pltpu.make_async_copy(v_source, v_own, own_sem.at[1])
-    k_copy.start()
+
+    def own_copies(source, target, which):
+        size = source.shape[0] // own_sem.shape[1]
+        return [
+            pltpu.make_async_copy(
+                source.at[pl.ds(chunk * size, size)],
+                target.at[pl.ds(chunk * size, size)],
+                own_sem.at[which, chunk],
+            )
+            for chunk in range(own_sem.shape[1])
+        ]
+
+    k_copies = own_copies(k_source, k_own, 0)
+    v_copies = own_copies(v_source, v_own, 1)
+    for copy in k_copies:
+        copy.start()
+
+    def end_k_start_v():
+        for copy in k_copies:
+            copy.wait()
+        for copy in v_copies:
+            copy.start()
+
+    def end_v():
+        for copy in v_copies:
+            copy.wait()
+
     pair_at = lax.axis_index("seq")
     is_retrieval, window_len, sink_len = look_up(table_ref)
     tokens = recv_ref.shape[0]
@@ -407,11 +431,10 @@
                     acc[row_at] = acc[row_at] + part_acc if row_at in acc else part_acc
 
         first(peer_blocks)
-        k_copy.wait()
-        v_copy.start()
+        end_k_start_v()
         first(own_blocks)
         second(peer_blocks)
-        v_copy.wait()
+        end_v()
         second(own_blocks)
         for row_at in row_starts:
             cols = slice(row_at, row_at + row_block)
@@ -451,11 +474,10 @@
                     work(index)
 
         each(first, peer_blocks)
-        k_copy.wait()
-        v_copy.start()
+        end_k_start_v()
         each(first, own_blocks)
         each(second, peer_blocks)
-        v_copy.wait()
+        end_v()
         each(second, own_blocks)
         top = jnp.max(stat_ref[0:8, :], axis=0, keepdims=True)
         stat_ref[0:8, :] = jnp.broadcast_to(top, (8, rows))
@@ -509,7 +531,7 @@
             pltpu.VMEM((ctx_dev, head_dim), jnp.bfloat16),
             pltpu.VMEM((ctx_dev, head_dim), jnp.bfloat16),
             pltpu.VMEM((keys, rows), jnp.float32),
-            pltpu.SemaphoreType.DMA((2,)),
+            pltpu.SemaphoreType.DMA((2, 4)),
         ],
         compiler_params=pltpu.CompilerParams(vmem_limit_bytes=51 * 2**20),
     )(table, recv, k_peer, v_peer, k_own, v_own)

time: 36.2 us -> 36.5 us (level)
  blocking collectives: 25.8 us -> 26.4 us
  Pallas kernels: 8.58 us -> 8.01 us
    all_to_all x1, blocking collectives: 10.6 us -> 11.2 us  [on_device_pairs(): lax.all_to_all(result, 'head', split_axis=0, concat_axis=0, tiled=True)]
    pallas_call x1, Pallas kernels: 5.68 us -> 5.11 us  [on_device_pairs(): pl.pallas_call(functools.partial(attend_kernel, tok_rows=tok_rows, group_...]
  transfers between devices with their start and end apart: 3 -> 3, of which waited for: 0 -> 0; matrix products, arithmetic and copies ran while one was open for 3% -> 3% of each run, Pallas kernels for 17% -> 16%
where the time goes in v4:
time: 36.5 us; the launch traced here: 36.2 us
  blocking collectives  26.4 us (72%)
  Pallas kernels  8.01 us (22%)
  other arithmetic  1.04 us (3%)
  starting transfers between devices  0.58 us (2%)
    all_to_all x1, blocking collectives, on_device_pairs(): recv = lax.all_to_all(send, 'head', split_axis=0, concat_axis=0, tiled=True)  15.2 us
    all_to_all x1, blocking collectives, on_device_pairs(): lax.all_to_all(result, 'head', split_axis=0, concat_axis=0, tiled=True)  11.2 us
    pallas_call x1, Pallas kernels, on_device_pairs(): pl.pallas_call(functools.partial(attend_kernel, tok_rows=tok_rows, group_...  5.11 us
    pallas_call x1, Pallas kernels, on_device_pairs(): pl.pallas_call(unpack_kernel, out_shape=jax.ShapeDtypeStruct((tok_rows, K...  1.26 us
    pallas_call x1, Pallas kernels, on_device_pairs(): pl.pallas_call(functools.partial(span_kernel, tok_rows=tok_rows, group_he...  1.07 us
    concatenate x1, other arithmetic, on_device_pairs(): joined = jnp.concatenate([q_span, k_span, v_span], axis=1)  0.96 us
  transfers between devices with their start and end apart: 3, of which 0 were waited for; matrix products, arithmetic and copies ran while one was open for 3% of the time, Pallas kernels for 16%

profile of v4, /device:TPU:0, one launch (start us, length us, event | category | flops | bytes accessed | tf_op | source)
XLA Modules:
  0.0 36.2 jit_solution(1767187257106002571)
XLA Ops:
  0.0 0.5 %collective-permute-start.1 = (bf16[4096,128]{1,0:T(8,128)(2,1)}, bf16[4096,128]{1,0:T(8,128)(2,1)S(1)}, u32[]{:S(2)}, u32[]{:S(2)}) collective-permute-start(bf16[4096,128]{1,0:T(8,128)(2,1)} %bitcast.8), channel_id=1, source_target_pairs={{0,1},{1,0},{2,3},{3,2},{4,5},{5,4},{6,7},{7,6},{8,9},{9,8},{10,11... | collective-permute-start | bytes 3145736 | tf_op jit(solution)/shard_map/ppermute | solution.py:497
  0.5 0.0 copy-start
  0.5 0.0 copy-start.1
  0.5 0.0 copy-start.2
  0.5 0.0 copy-start.3
  0.5 0.1 collective-permute-start.2
  0.6 1.0 %pad_maximum_fusion.in_ref = bf16[16,6144]{1,0:T(8,128)(2,1)S(1)} fusion(bf16[16,1024]{1,0:T(8,128)(2,1)} %param.11, bf16[16,1024]{1,0:T(8,128)(2,1)} %param.10, bf16[16,4096]{1,0:T(8,128)(2,1)} %param.9), kind=kLoop, calls=%fused_computation | loop fusion | flops 589824 | bytes 393216 | tf_op jit(solution)/shard_map/concatenate | solution.py:499
  1.5 0.0 copy-done
  1.6 0.0 copy-done.1
  1.6 0.0 copy-done.2
  1.6 0.0 copy-done.3
  1.6 0.1 pad_add_fusion.head_ref.table_ref
  1.7 0.6 %shard_map.91 = bf16[8,16,768]{2,1,0:T(8,128)(2,1)S(1)} custom-call(s32[32]{0:T(128)S(1)} %pad_add_fusion.head_ref.table_ref, bf16[16,6144]{1,0:T(8,128)(2,1)S(1)} %pad_maximum_fusion.in_ref), custom_call_target="tpu_custom_call" | custom-call | tf_op jit(solution)/shard_map/pallas_call | solution.py:502
  2.2 15.2 %all_to_all.10 = bf16[8,16,768]{2,1,0:T(8,128)(2,1)S(1)} all-to-all(bf16[8,16,768]{2,1,0:T(8,128)(2,1)S(1)} %shard_map.91), channel_id=1, replica_groups=mesh['rep'=2,'head'=8,'seq'=2] {'head'}, dimensions={0} | all-to-all | bytes 393216 | tf_op jit(solution)/shard_map/all_to_all | solution.py:509
  17.5 0.0 collective-permute-start
  17.5 0.0 collective-permute-done.1.k_peer
  17.5 0.0 collective-permute-done.2.v_peer
  17.5 5.1 %shard_map.92 = (f32[128,512]{1,0:T(8,128)S(1)}, f32[16,512]{1,0:T(8,128)S(1)}) custom-call(s32[32]{0:T(128)S(1)} %pad_add_fusion.head_ref.table_ref, bf16[128,768]{1,0:T(8,128)(2,1)S(1)} %bitcast.5, bf16[4096,128]{1,0:T(8,128)(2,1)S(1)} %collective-permute-done.1.k_peer, bf16[4096,128]{1,0:T(8,128)(2,1)S(1)} %collective-permute-done.2.v_peer, ...), custom_call_target="tpu_custom_call" | custom-call | tf_op jit(solution)/shard_map/pallas_call | solution.py:515
  22.6 0.0 collective-permute-done.peer_ref
  22.6 1.1 %shard_map.93 = bf16[128,512]{1,0:T(8,128)(2,1)S(1)} custom-call(s32[32]{0:T(128)S(1)} %pad_add_fusion.head_ref.table_ref, bf16[128,768]{1,0:T(8,128)(2,1)S(1)} %bitcast.6, bf16[128,768]{1,0:T(8,128)(2,1)S(1)} %collective-permute-done.peer_ref, f32[128,512]{1,0:T(8,128)S(1)} %get-tuple-element.17.acc_ref, f32[16,512]{1,0:T(8,128)S(1)} %get-tuple-element.18.stat_ref), custom_call_target="tpu_custom_call" | custom-call | tf_op jit(solution)/shard_map/pallas_call | solution.py:538
  23.7 11.2 %all_to_all.11.in_ref = bf16[8,16,512]{2,1,0:T(8,128)(2,1)S(1)} all-to-all(bf16[8,16,512]{2,1,0:T(8,128)(2,1)S(1)} %bitcast.7), channel_id=1, replica_groups=mesh['rep'=2,'head'=8,'seq'=2] {'head'}, dimensions={0} | all-to-all | bytes 262144 | tf_op jit(solution)/shard_map/all_to_all | solution.py:552
  34.9 1.3 %shard_map.94 = bf16[16,4096]{1,0:T(8,128)(2,1)} custom-call(s32[32]{0:T(128)S(1)} %pad_add_fusion.head_ref.table_ref, bf16[8,16,512]{2,1,0:T(8,128)(2,1)S(1)} %all_to_all.11.in_ref), custom_call_target="tpu_custom_call" | custom-call | tf_op jit(solution)/shard_map/pallas_call | solution.py:553
Async XLA Ops:
  0.0 17.5 %collective-permute-start.1 = (bf16[4096,128]{1,0:T(8,128)(2,1)}, bf16[4096,128]{1,0:T(8,128)(2,1)S(1)}, u32[]{:S(2)}, u32[]{:S(2)}) collective-permute-start(bf16[4096,128]{1,0:T(8,128)(2,1)} %bitcast.8), channel_id=1, source_target_pairs={{0,1},{1,0},{2,3},{3,2},{4,5},{5,4},{6,7},{7,6},{8,9},{9,8},{10,11... | collective-permute-start | bytes 3145736 | tf_op jit(solution)/shard_map/ppermute | solution.py:497
  0.5 1.1 %copy-start = (s32[8]{0:T(128)S(1)}, s32[8]{0:T(128)}, u32[]{:S(2)}) copy-start(s32[8]{0:T(128)} %param.17) | copy-start | bytes 100
  0.5 1.1 %copy-start.1 = (s32[8]{0:T(128)S(1)}, s32[8]{0:T(128)}, u32[]{:S(2)}) copy-start(s32[8]{0:T(128)} %param.16) | copy-start | bytes 100
  0.5 1.1 %copy-start.2 = (s32[8]{0:T(128)S(1)}, s32[8]{0:T(128)}, u32[]{:S(2)}) copy-start(s32[8]{0:T(128)} %param.15) | copy-start | bytes 100
  0.5 1.1 %copy-start.3 = (s32[8]{0:T(128)S(1)}, s32[8]{0:T(128)}, u32[]{:S(2)}) copy-start(s32[8]{0:T(128)} %param.14) | copy-start | bytes 100
  0.5 17.0 %collective-permute-start.2 = (bf16[4096,128]{1,0:T(8,128)(2,1)}, bf16[4096,128]{1,0:T(8,128)(2,1)S(1)}, u32[]{:S(2)}, u32[]{:S(2)}) collective-permute-start(bf16[4096,128]{1,0:T(8,128)(2,1)} %bitcast.10), channel_id=1, source_target_pairs={{0,1},{1,0},{2,3},{3,2},{4,5},{5,4},{6,7},{7,6},{8,9},{9,8},{10,11... | collective-permute-start | bytes 3145736 | tf_op jit(solution)/shard_map/ppermute | solution.py:498
  17.5 5.1 %collective-permute-start = (bf16[128,768]{1,0:T(8,128)(2,1)S(1)}, bf16[128,768]{1,0:T(8,128)(2,1)S(1)}, u32[]{:S(2)}, u32[]{:S(2)}) collective-permute-start(bf16[128,768]{1,0:T(8,128)(2,1)S(1)} %bitcast.4), channel_id=1, source_target_pairs={{0,1},{1,0},{2,3},{3,2},{4,5},{5,4},{6,7},{7,6},{8,9},{9,8},{10,11... | collective-permute-start | bytes 589832 | tf_op jit(solution)/shard_map/ppermute | solution.py:511

commit v5 on v4

--- a/solution.py
+++ b/solution.py
@@ -338,82 +338,84 @@
 
     span_k = pl.ds(group_width, head_dim)
     span_v = pl.ds(group_width + head_dim, head_dim)
-    cached, spans = [], []
-    for k_ref, v_ref, pair in ((k_peer, v_peer, 1 - pair_at), (k_own, v_own, pair_at)):
-        for start in range(0, ctx_dev, key_block):
-            cached.append((k_ref, v_ref, start, key_block, pair))
-    spans.append((recv_ref, pair_at))
-
-    def load_keys(index):
-        if index < len(cached):
-            k_ref, _, start, size, _ = cached[index]
-            return k_ref[start : start + size, :]
-        return spans[index - len(cached)][0][:, span_k]
-
-    def load_values(index):
-        if index < len(cached):
-            _, v_ref, start, size, _ = cached[index]
-            return v_ref[start : start + size, :]
-        return spans[index - len(cached)][0][:, span_v]
-
-    def place(index):
-        if index < len(cached):
-            return index * key_block, key_block
-        return len(cached) * key_block + (index - len(cached)) * tokens, tokens
-
-    def first_pos(index):
-        _, _, start, _, pair = cached[index]
-        return pair * ctx_dev + start
-
-    def scores(index, row_at, masked):
-        keys = load_keys(index)
-        keys = jnp.concatenate([keys, keys], axis=1)
-        block = lax.dot_general(
-            keys,
-            queries[row_at : row_at + row_block],
-            (((1,), (1,)), ((), ())),
-            preferred_element_type=f32,
-        )
-        size = block.shape[0]
-        pos_q = query_pos[:, row_at : row_at + row_block]
-        column = lax.broadcasted_iota(jnp.int32, (size, 1), 0)
-        allowed = None
-        if index >= len(cached):
-            pos_k = token_pos(column, spans[index - len(cached)][1])
-            allowed = pos_k <= pos_q
-        else:
-            pos_k = first_pos(index) + column
-        if masked:
-            near = (pos_k < sink_len) | (pos_k > pos_q - window_len)
-            allowed = near if allowed is None else allowed & near
-        if allowed is not None:
-            block = jnp.where(allowed, block, NEG_FILL)
-        start, _ = place(index)
-        score_ref[start : start + size, row_at : row_at + row_block] = block
-        return jnp.max(block.reshape(size // 8, 8, row_block), axis=0)
-
-    def weighted(index, row_at, top):
-        start, size = place(index)
-        block = score_ref[start : start + size, row_at : row_at + row_block]
-        weights = jnp.exp2(block - top)
-        total = jnp.sum(weights.reshape(size // 8, 8, row_block), axis=0)
-        acc = lax.dot_general(
-            load_values(index),
-            weights.astype(bf16),
-            (((0,), (0,)), ((), ())),
-            preferred_element_type=f32,
-        )
-        return total, acc
-
-    blocks = len(cached) + len(spans)
+
+    def build(key_block):
+        cached, spans = [], []
+        for k_ref, v_ref, pair in ((k_peer, v_peer, 1 - pair_at), (k_own, v_own, pair_at)):
+            for start in range(0, ctx_dev, key_block):
+                cached.append((k_ref, v_ref, start, key_block, pair))
+        spans.append((recv_ref, pair_at))
+
+        def load_keys(index):
+            if index < len(cached):
+                k_ref, _, start, size, _ = cached[index]
+                return k_ref[start : start + size, :]
+            return spans[index - len(cached)][0][:, span_k]
+
+        def load_values(index):
+            if index < len(cached):
+                _, v_ref, start, size, _ = cached[index]
+                return v_ref[start : start + size, :]
+            return spans[index - len(cached)][0][:, span_v]
+
+        def place(index):
+            if index < len(cached):
+                return index * key_block, key_block
+            return len(cached) * key_block + (index - len(cached)) * tokens, tokens
+
+        def first_pos(index):
+            _, _, start, _, pair = cached[index]
+            return pair * ctx_dev + start
+
+        def scores(index, row_at, masked):
+            keys = load_keys(index)
+            keys = jnp.concatenate([keys, keys], axis=1)
+            block = lax.dot_general(
+                keys,
+                queries[row_at : row_at + row_block],
+                (((1,), (1,)), ((), ())),
+                preferred_element_type=f32,
+            )
+            size = block.shape[0]
+            pos_q = query_pos[:, row_at : row_at + row_block]
+            column = lax.broadcasted_iota(jnp.int32, (size, 1), 0)
+            allowed = None
+            if index >= len(cached):
+                pos_k = token_pos(column, spans[index - len(cached)][1])
+                allowed = pos_k <= pos_q
+            else:
+                pos_k = first_pos(index) + column
+            if masked:
+                near = (pos_k < sink_len) | (pos_k > pos_q - window_len)
+                allowed = near if allowed is None else allowed & near
+            if allowed is not None:
+                block = jnp.where(allowed, block, NEG_FILL)
+            start, _ = place(index)
+            score_ref[start : start + size, row_at : row_at + row_block] = block
+            return jnp.max(block.reshape(size // 8, 8, row_block), axis=0)
+
+        def weighted(index, row_at, top):
+            start, size = place(index)
+            block = score_ref[start : start + size, row_at : row_at + row_block]
+            weights = jnp.exp2(block - top)
+            total = jnp.sum(weights.reshape(size // 8, 8, row_block), axis=0)
+            acc = lax.dot_general(
+                load_values(index),
+                weights.astype(bf16),
+                (((0,), (0,)), ((), ())),
+                preferred_element_type=f32,
+            )
+            return total, acc
+
+        return len(cached), len(spans), first_pos, scores, weighted
+
     row_starts = list(range(0, rows, row_block))
-
-    half = len(cached) // 2
-    peer_blocks = list(range(half))
-    own_blocks = list(range(half, blocks))
 
     @pl.when(is_retrieval == 1)
     def _():
+        cached, spans, _, scores, weighted = build(ctx_dev)
+        peer_blocks = list(range(cached // 2))
+        own_blocks = list(range(cached // 2, cached + spans))
         running, total, acc = {}, {}, {}
 
         def first(indices):
@@ -445,6 +447,10 @@
 
     @pl.when(is_retrieval != 1)
     def _():
+        cached, spans, first_pos, scores, weighted = build(key_block)
+        peer_blocks = list(range(cached // 2))
+        own_blocks = list(range(cached // 2, cached + spans))
+
         def needed(index):
             pos = first_pos(index)
             return (pos < sink_len) | (pos + key_block - 1 > context - window_len)
@@ -468,7 +474,7 @@
 
         def each(work, indices):
             for index in indices:
-                if index < len(cached):
+                if index < cached:
                     pl.when(needed(index))(functools.partial(work, index))
                 else:
                     work(index)

time: 36.5 us -> 37.2 us (1.019)
  Pallas kernels: 8.01 us -> 8.98 us
    pallas_call x1, Pallas kernels: 5.11 us -> 6.08 us  [on_device_pairs(): pl.pallas_call(functools.partial(attend_kernel, tok_rows=tok_rows, group_...]
  transfers between devices with their start and end apart: 3 -> 3, of which waited for: 0 -> 0; matrix products, arithmetic and copies ran while one was open for 3% -> 3% of each run, Pallas kernels for 16% -> 18%
where the time goes in v5:
time: 37.2 us
  blocking collectives  26.5 us (71%)
  Pallas kernels  8.98 us (24%)
  other arithmetic  1.04 us (3%)
  starting transfers between devices  0.58 us (2%)
    all_to_all x1, blocking collectives, on_device_pairs(): recv = lax.all_to_all(send, 'head', split_axis=0, concat_axis=0, tiled=True)  15.2 us
    all_to_all x1, blocking collectives, on_device_pairs(): lax.all_to_all(result, 'head', split_axis=0, concat_axis=0, tiled=True)  11.3 us
    pallas_call x1, Pallas kernels, on_device_pairs(): pl.pallas_call(functools.partial(attend_kernel, tok_rows=tok_rows, group_...  6.08 us
    pallas_call x1, Pallas kernels, on_device_pairs(): pl.pallas_call(unpack_kernel, out_shape=jax.ShapeDtypeStruct((tok_rows, K...  1.26 us
    pallas_call x1, Pallas kernels, on_device_pairs(): pl.pallas_call(functools.partial(span_kernel, tok_rows=tok_rows, group_he...  1.07 us
    concatenate x1, other arithmetic, on_device_pairs(): joined = jnp.concatenate([q_span, k_span, v_span], axis=1)  0.96 us
  transfers between devices with their start and end apart: 3, of which 0 were waited for; matrix products, arithmetic and copies ran while one was open for 3% of the time, Pallas kernels for 18%

profile of v5, /device:TPU:0, one launch (start us, length us, event | category | flops | bytes accessed | tf_op | source)
XLA Modules:
  0.0 37.2 jit_solution(851381401516824447)
XLA Ops:
  0.0 0.5 %collective-permute-start.1 = (bf16[4096,128]{1,0:T(8,128)(2,1)}, bf16[4096,128]{1,0:T(8,128)(2,1)S(1)}, u32[]{:S(2)}, u32[]{:S(2)}) collective-permute-start(bf16[4096,128]{1,0:T(8,128)(2,1)} %bitcast.8), channel_id=1, source_target_pairs={{0,1},{1,0},{2,3},{3,2},{4,5},{5,4},{6,7},{7,6},{8,9},{9,8},{10,11... | collective-permute-start | bytes 3145736 | tf_op jit(solution)/shard_map/ppermute | solution.py:503
  0.5 0.0 copy-start
  0.5 0.0 copy-start.1
  0.5 0.0 copy-start.2
  0.5 0.0 copy-start.3
  0.5 0.1 collective-permute-start.2
  0.6 1.0 %pad_maximum_fusion.in_ref = bf16[16,6144]{1,0:T(8,128)(2,1)S(1)} fusion(bf16[16,1024]{1,0:T(8,128)(2,1)} %param.11, bf16[16,1024]{1,0:T(8,128)(2,1)} %param.10, bf16[16,4096]{1,0:T(8,128)(2,1)} %param.9), kind=kLoop, calls=%fused_computation | loop fusion | flops 589824 | bytes 393216 | tf_op jit(solution)/shard_map/concatenate | solution.py:505
  1.5 0.0 copy-done
  1.6 0.0 copy-done.1
  1.6 0.0 copy-done.2
  1.6 0.0 copy-done.3
  1.6 0.1 pad_add_fusion.head_ref.table_ref
  1.7 0.6 %shard_map.91 = bf16[8,16,768]{2,1,0:T(8,128)(2,1)S(1)} custom-call(s32[32]{0:T(128)S(1)} %pad_add_fusion.head_ref.table_ref, bf16[16,6144]{1,0:T(8,128)(2,1)S(1)} %pad_maximum_fusion.in_ref), custom_call_target="tpu_custom_call" | custom-call | tf_op jit(solution)/shard_map/pallas_call | solution.py:508
  2.2 15.2 %all_to_all.10 = bf16[8,16,768]{2,1,0:T(8,128)(2,1)S(1)} all-to-all(bf16[8,16,768]{2,1,0:T(8,128)(2,1)S(1)} %shard_map.91), channel_id=1, replica_groups=mesh['rep'=2,'head'=8,'seq'=2] {'head'}, dimensions={0} | all-to-all | bytes 393216 | tf_op jit(solution)/shard_map/all_to_all | solution.py:515
  17.5 0.0 collective-permute-start
  17.5 0.0 collective-permute-done.1.k_peer
  17.5 0.0 collective-permute-done.2.v_peer
  17.5 6.1 %shard_map.92 = (f32[128,512]{1,0:T(8,128)S(1)}, f32[16,512]{1,0:T(8,128)S(1)}) custom-call(s32[32]{0:T(128)S(1)} %pad_add_fusion.head_ref.table_ref, bf16[128,768]{1,0:T(8,128)(2,1)S(1)} %bitcast.5, bf16[4096,128]{1,0:T(8,128)(2,1)S(1)} %collective-permute-done.1.k_peer, bf16[4096,128]{1,0:T(8,128)(2,1)S(1)} %collective-permute-done.2.v_peer, ...), custom_call_target="tpu_custom_call" | custom-call | tf_op jit(solution)/shard_map/pallas_call | solution.py:521
  23.6 0.0 collective-permute-done.peer_ref
  23.6 1.1 %shard_map.93 = bf16[128,512]{1,0:T(8,128)(2,1)S(1)} custom-call(s32[32]{0:T(128)S(1)} %pad_add_fusion.head_ref.table_ref, bf16[128,768]{1,0:T(8,128)(2,1)S(1)} %bitcast.6, bf16[128,768]{1,0:T(8,128)(2,1)S(1)} %collective-permute-done.peer_ref, f32[128,512]{1,0:T(8,128)S(1)} %get-tuple-element.17.acc_ref, f32[16,512]{1,0:T(8,128)S(1)} %get-tuple-element.18.stat_ref), custom_call_target="tpu_custom_call" | custom-call | tf_op jit(solution)/shard_map/pallas_call | solution.py:544
  24.6 11.3 %all_to_all.11.in_ref = bf16[8,16,512]{2,1,0:T(8,128)(2,1)S(1)} all-to-all(bf16[8,16,512]{2,1,0:T(8,128)(2,1)S(1)} %bitcast.7), channel_id=1, replica_groups=mesh['rep'=2,'head'=8,'seq'=2] {'head'}, dimensions={0} | all-to-all | bytes 262144 | tf_op jit(solution)/shard_map/all_to_all | solution.py:558
  35.9 1.3 %shard_map.94 = bf16[16,4096]{1,0:T(8,128)(2,1)} custom-call(s32[32]{0:T(128)S(1)} %pad_add_fusion.head_ref.table_ref, bf16[8,16,512]{2,1,0:T(8,128)(2,1)S(1)} %all_to_all.11.in_ref), custom_call_target="tpu_custom_call" | custom-call | tf_op jit(solution)/shard_map/pallas_call | solution.py:559
Async XLA Ops:
  0.0 17.5 %collective-permute-start.1 = (bf16[4096,128]{1,0:T(8,128)(2,1)}, bf16[4096,128]{1,0:T(8,128)(2,1)S(1)}, u32[]{:S(2)}, u32[]{:S(2)}) collective-permute-start(bf16[4096,128]{1,0:T(8,128)(2,1)} %bitcast.8), channel_id=1, source_target_pairs={{0,1},{1,0},{2,3},{3,2},{4,5},{5,4},{6,7},{7,6},{8,9},{9,8},{10,11... | collective-permute-start | bytes 3145736 | tf_op jit(solution)/shard_map/ppermute | solution.py:503
  0.5 1.1 %copy-start = (s32[8]{0:T(128)S(1)}, s32[8]{0:T(128)}, u32[]{:S(2)}) copy-start(s32[8]{0:T(128)} %param.17) | copy-start | bytes 100
  0.5 1.1 %copy-start.1 = (s32[8]{0:T(128)S(1)}, s32[8]{0:T(128)}, u32[]{:S(2)}) copy-start(s32[8]{0:T(128)} %param.16) | copy-start | bytes 100
  0.5 1.1 %copy-start.2 = (s32[8]{0:T(128)S(1)}, s32[8]{0:T(128)}, u32[]{:S(2)}) copy-start(s32[8]{0:T(128)} %param.15) | copy-start | bytes 100
  0.5 1.1 %copy-start.3 = (s32[8]{0:T(128)S(1)}, s32[8]{0:T(128)}, u32[]{:S(2)}) copy-start(s32[8]{0:T(128)} %param.14) | copy-start | bytes 100
  0.5 17.0 %collective-permute-start.2 = (bf16[4096,128]{1,0:T(8,128)(2,1)}, bf16[4096,128]{1,0:T(8,128)(2,1)S(1)}, u32[]{:S(2)}, u32[]{:S(2)}) collective-permute-start(bf16[4096,128]{1,0:T(8,128)(2,1)} %bitcast.10), channel_id=1, source_target_pairs={{0,1},{1,0},{2,3},{3,2},{4,5},{5,4},{6,7},{7,6},{8,9},{9,8},{10,11... | collective-permute-start | bytes 3145736 | tf_op jit(solution)/shard_map/ppermute | solution.py:504
  17.5 6.1 %collective-permute-start = (bf16[128,768]{1,0:T(8,128)(2,1)S(1)}, bf16[128,768]{1,0:T(8,128)(2,1)S(1)}, u32[]{:S(2)}, u32[]{:S(2)}) collective-permute-start(bf16[128,768]{1,0:T(8,128)(2,1)S(1)} %bitcast.4), channel_id=1, source_target_pairs={{0,1},{1,0},{2,3},{3,2},{4,5},{5,4},{6,7},{7,6},{8,9},{9,8},{10,11... | collective-permute-start | bytes 589832 | tf_op jit(solution)/shard_map/ppermute | solution.py:517

commit v6 on v5

--- a/solution.py
+++ b/solution.py
@@ -413,7 +413,7 @@
 
     @pl.when(is_retrieval == 1)
     def _():
-        cached, spans, _, scores, weighted = build(ctx_dev)
+        cached, spans, _, scores, weighted = build(math.gcd(ctx_dev, 512))
         peer_blocks = list(range(cached // 2))
         own_blocks = list(range(cached // 2, cached + spans))
         running, total, acc = {}, {}, {}

time: 37.2 us -> 36.5 us (0.981)
  blocking collectives: 26.5 us -> 25.8 us
  Pallas kernels: 8.98 us -> 8.59 us
    all_to_all x1, blocking collectives: 11.3 us -> 10.6 us  [on_device_pairs(): lax.all_to_all(result, 'head', split_axis=0, concat_axis=0, tiled=True)]
    pallas_call x1, Pallas kernels: 6.08 us -> 5.7 us  [on_device_pairs(): pl.pallas_call(functools.partial(attend_kernel, tok_rows=tok_rows, group_...]
  transfers between devices with their start and end apart: 3 -> 3, of which waited for: 0 -> 0; matrix products, arithmetic and copies ran while one was open for 3% -> 3% of each run, Pallas kernels for 18% -> 17%
where the time goes in v6:
time: 36.5 us; the launch traced here: 36.1 us
  blocking collectives  25.8 us (71%)
  Pallas kernels  8.59 us (24%)
  other arithmetic  1.04 us (3%)
  starting transfers between devices  0.58 us (2%)
    all_to_all x1, blocking collectives, on_device_pairs(): recv = lax.all_to_all(send, 'head', split_axis=0, concat_axis=0, tiled=True)  15.2 us
    all_to_all x1, blocking collectives, on_device_pairs(): lax.all_to_all(result, 'head', split_axis=0, concat_axis=0, tiled=True)  10.6 us
    pallas_call x1, Pallas kernels, on_device_pairs(): pl.pallas_call(functools.partial(attend_kernel, tok_rows=tok_rows, group_...  5.7 us
    pallas_call x1, Pallas kernels, on_device_pairs(): pl.pallas_call(unpack_kernel, out_shape=jax.ShapeDtypeStruct((tok_rows, K...  1.26 us
    pallas_call x1, Pallas kernels, on_device_pairs(): pl.pallas_call(functools.partial(span_kernel, tok_rows=tok_rows, group_he...  1.07 us
    concatenate x1, other arithmetic, on_device_pairs(): joined = jnp.concatenate([q_span, k_span, v_span], axis=1)  0.96 us
  transfers between devices with their start and end apart: 3, of which 0 were waited for; matrix products, arithmetic and copies ran while one was open for 3% of the time, Pallas kernels for 17%

profile of v6, /device:TPU:0, one launch (start us, length us, event | category | flops | bytes accessed | tf_op | source)
XLA Modules:
  0.0 36.1 jit_solution(3803054905067282696)
XLA Ops:
  0.0 0.5 %collective-permute-start.1 = (bf16[4096,128]{1,0:T(8,128)(2,1)}, bf16[4096,128]{1,0:T(8,128)(2,1)S(1)}, u32[]{:S(2)}, u32[]{:S(2)}) collective-permute-start(bf16[4096,128]{1,0:T(8,128)(2,1)} %bitcast.8), channel_id=1, source_target_pairs={{0,1},{1,0},{2,3},{3,2},{4,5},{5,4},{6,7},{7,6},{8,9},{9,8},{10,11... | collective-permute-start | bytes 3145736 | tf_op jit(solution)/shard_map/ppermute | solution.py:503
  0.5 0.0 copy-start
  0.5 0.0 copy-start.1
  0.5 0.0 copy-start.2
  0.5 0.0 copy-start.3
  0.5 0.1 collective-permute-start.2
  0.6 1.0 %pad_maximum_fusion.in_ref = bf16[16,6144]{1,0:T(8,128)(2,1)S(1)} fusion(bf16[16,1024]{1,0:T(8,128)(2,1)} %param.11, bf16[16,1024]{1,0:T(8,128)(2,1)} %param.10, bf16[16,4096]{1,0:T(8,128)(2,1)} %param.9), kind=kLoop, calls=%fused_computation | loop fusion | flops 589824 | bytes 393216 | tf_op jit(solution)/shard_map/concatenate | solution.py:505
  1.5 0.0 copy-done
  1.6 0.0 copy-done.1
  1.6 0.0 copy-done.2
  1.6 0.0 copy-done.3
  1.6 0.1 pad_add_fusion.head_ref.table_ref
  1.7 0.6 %shard_map.91 = bf16[8,16,768]{2,1,0:T(8,128)(2,1)S(1)} custom-call(s32[32]{0:T(128)S(1)} %pad_add_fusion.head_ref.table_ref, bf16[16,6144]{1,0:T(8,128)(2,1)S(1)} %pad_maximum_fusion.in_ref), custom_call_target="tpu_custom_call" | custom-call | tf_op jit(solution)/shard_map/pallas_call | solution.py:508
  2.2 15.2 %all_to_all.10 = bf16[8,16,768]{2,1,0:T(8,128)(2,1)S(1)} all-to-all(bf16[8,16,768]{2,1,0:T(8,128)(2,1)S(1)} %shard_map.91), channel_id=1, replica_groups=mesh['rep'=2,'head'=8,'seq'=2] {'head'}, dimensions={0} | all-to-all | bytes 393216 | tf_op jit(solution)/shard_map/all_to_all | solution.py:515
  17.5 0.0 collective-permute-start
  17.5 0.0 collective-permute-done.1.k_peer
  17.5 0.0 collective-permute-done.2.v_peer
  17.5 5.7 %shard_map.92 = (f32[128,512]{1,0:T(8,128)S(1)}, f32[16,512]{1,0:T(8,128)S(1)}) custom-call(s32[32]{0:T(128)S(1)} %pad_add_fusion.head_ref.table_ref, bf16[128,768]{1,0:T(8,128)(2,1)S(1)} %bitcast.5, bf16[4096,128]{1,0:T(8,128)(2,1)S(1)} %collective-permute-done.1.k_peer, bf16[4096,128]{1,0:T(8,128)(2,1)S(1)} %collective-permute-done.2.v_peer, ...), custom_call_target="tpu_custom_call" | custom-call | tf_op jit(solution)/shard_map/pallas_call | solution.py:521
  23.2 0.0 collective-permute-done.peer_ref
  23.2 1.1 %shard_map.93 = bf16[128,512]{1,0:T(8,128)(2,1)S(1)} custom-call(s32[32]{0:T(128)S(1)} %pad_add_fusion.head_ref.table_ref, bf16[128,768]{1,0:T(8,128)(2,1)S(1)} %bitcast.6, bf16[128,768]{1,0:T(8,128)(2,1)S(1)} %collective-permute-done.peer_ref, f32[128,512]{1,0:T(8,128)S(1)} %get-tuple-element.17.acc_ref, f32[16,512]{1,0:T(8,128)S(1)} %get-tuple-element.18.stat_ref), custom_call_target="tpu_custom_call" | custom-call | tf_op jit(solution)/shard_map/pallas_call | solution.py:544
  24.3 10.6 %all_to_all.11.in_ref = bf16[8,16,512]{2,1,0:T(8,128)(2,1)S(1)} all-to-all(bf16[8,16,512]{2,1,0:T(8,128)(2,1)S(1)} %bitcast.7), channel_id=1, replica_groups=mesh['rep'=2,'head'=8,'seq'=2] {'head'}, dimensions={0} | all-to-all | bytes 262144 | tf_op jit(solution)/shard_map/all_to_all | solution.py:558
  34.9 1.3 %shard_map.94 = bf16[16,4096]{1,0:T(8,128)(2,1)} custom-call(s32[32]{0:T(128)S(1)} %pad_add_fusion.head_ref.table_ref, bf16[8,16,512]{2,1,0:T(8,128)(2,1)S(1)} %all_to_all.11.in_ref), custom_call_target="tpu_custom_call" | custom-call | tf_op jit(solution)/shard_map/pallas_call | solution.py:559
Async XLA Ops:
  0.0 17.5 %collective-permute-start.1 = (bf16[4096,128]{1,0:T(8,128)(2,1)}, bf16[4096,128]{1,0:T(8,128)(2,1)S(1)}, u32[]{:S(2)}, u32[]{:S(2)}) collective-permute-start(bf16[4096,128]{1,0:T(8,128)(2,1)} %bitcast.8), channel_id=1, source_target_pairs={{0,1},{1,0},{2,3},{3,2},{4,5},{5,4},{6,7},{7,6},{8,9},{9,8},{10,11... | collective-permute-start | bytes 3145736 | tf_op jit(solution)/shard_map/ppermute | solution.py:503
  0.5 1.1 %copy-start = (s32[8]{0:T(128)S(1)}, s32[8]{0:T(128)}, u32[]{:S(2)}) copy-start(s32[8]{0:T(128)} %param.17) | copy-start | bytes 100
  0.5 1.1 %copy-start.1 = (s32[8]{0:T(128)S(1)}, s32[8]{0:T(128)}, u32[]{:S(2)}) copy-start(s32[8]{0:T(128)} %param.16) | copy-start | bytes 100
  0.5 1.1 %copy-start.2 = (s32[8]{0:T(128)S(1)}, s32[8]{0:T(128)}, u32[]{:S(2)}) copy-start(s32[8]{0:T(128)} %param.15) | copy-start | bytes 100
  0.5 1.1 %copy-start.3 = (s32[8]{0:T(128)S(1)}, s32[8]{0:T(128)}, u32[]{:S(2)}) copy-start(s32[8]{0:T(128)} %param.14) | copy-start | bytes 100
  0.5 17.0 %collective-permute-start.2 = (bf16[4096,128]{1,0:T(8,128)(2,1)}, bf16[4096,128]{1,0:T(8,128)(2,1)S(1)}, u32[]{:S(2)}, u32[]{:S(2)}) collective-permute-start(bf16[4096,128]{1,0:T(8,128)(2,1)} %bitcast.10), channel_id=1, source_target_pairs={{0,1},{1,0},{2,3},{3,2},{4,5},{5,4},{6,7},{7,6},{8,9},{9,8},{10,11... | collective-permute-start | bytes 3145736 | tf_op jit(solution)/shard_map/ppermute | solution.py:504
  17.5 5.7 %collective-permute-start = (bf16[128,768]{1,0:T(8,128)(2,1)S(1)}, bf16[128,768]{1,0:T(8,128)(2,1)S(1)}, u32[]{:S(2)}, u32[]{:S(2)}) collective-permute-start(bf16[128,768]{1,0:T(8,128)(2,1)S(1)} %bitcast.4), channel_id=1, source_target_pairs={{0,1},{1,0},{2,3},{3,2},{4,5},{5,4},{6,7},{7,6},{8,9},{9,8},{10,11... | collective-permute-start | bytes 589832 | tf_op jit(solution)/shard_map/ppermute | solution.py:517

commit v7 on v6

--- a/solution.py
+++ b/solution.py
@@ -516,7 +516,7 @@
     recv = recv.reshape(tokens, group_width + 2 * head_dim)
     peer = lax.ppermute(recv, "seq", swap)
     key_block = math.gcd(ctx_dev, 1024)
-    row_block = 256
+    row_block = rows
     keys = 2 * ctx_dev + tokens
     acc, stat = pl.pallas_call(
         functools.partial(

time: 36.5 us -> 37.1 us (1.016)
  Pallas kernels: 8.59 us -> 9.27 us
    pallas_call x1, Pallas kernels: 5.7 us -> 6.37 us  [on_device_pairs(): pl.pallas_call(functools.partial(attend_kernel, tok_rows=tok_rows, group_...]
  transfers between devices with their start and end apart: 3 -> 3, of which waited for: 0 -> 0; matrix products, arithmetic and copies ran while one was open for 3% -> 3% of each run, Pallas kernels for 17% -> 19%
where the time goes in v7:
time: 37.1 us; the launch traced here: 36.8 us
  blocking collectives  25.8 us (70%)
  Pallas kernels  9.27 us (25%)
  other arithmetic  1.04 us (3%)
  starting transfers between devices  0.58 us (2%)
    all_to_all x1, blocking collectives, on_device_pairs(): recv = lax.all_to_all(send, 'head', split_axis=0, concat_axis=0, tiled=True)  15.2 us
    all_to_all x1, blocking collectives, on_device_pairs(): lax.all_to_all(result, 'head', split_axis=0, concat_axis=0, tiled=True)  10.6 us
    pallas_call x1, Pallas kernels, on_device_pairs(): pl.pallas_call(functools.partial(attend_kernel, tok_rows=tok_rows, group_...  6.37 us
    pallas_call x1, Pallas kernels, on_device_pairs(): pl.pallas_call(unpack_kernel, out_shape=jax.ShapeDtypeStruct((tok_rows, K...  1.26 us
    pallas_call x1, Pallas kernels, on_device_pairs(): pl.pallas_call(functools.partial(span_kernel, tok_rows=tok_rows, group_he...  1.07 us
    concatenate x1, other arithmetic, on_device_pairs(): joined = jnp.concatenate([q_span, k_span, v_span], axis=1)  0.96 us
  transfers between devices with their start and end apart: 3, of which 0 were waited for; matrix products, arithmetic and copies ran while one was open for 3% of the time, Pallas kernels for 19%

profile of v7, /device:TPU:0, one launch (start us, length us, event | category | flops | bytes accessed | tf_op | source)
XLA Modules:
  0.0 36.8 jit_solution(3543535678744464323)
XLA Ops:
  0.0 0.5 %collective-permute-start.1 = (bf16[4096,128]{1,0:T(8,128)(2,1)}, bf16[4096,128]{1,0:T(8,128)(2,1)S(1)}, u32[]{:S(2)}, u32[]{:S(2)}) collective-permute-start(bf16[4096,128]{1,0:T(8,128)(2,1)} %bitcast.8), channel_id=1, source_target_pairs={{0,1},{1,0},{2,3},{3,2},{4,5},{5,4},{6,7},{7,6},{8,9},{9,8},{10,11... | collective-permute-start | bytes 3145736 | tf_op jit(solution)/shard_map/ppermute | solution.py:503
  0.5 0.0 copy-start
  0.5 0.0 copy-start.1
  0.5 0.0 copy-start.2
  0.5 0.0 copy-start.3
  0.5 0.1 collective-permute-start.2
  0.6 1.0 %pad_maximum_fusion.in_ref = bf16[16,6144]{1,0:T(8,128)(2,1)S(1)} fusion(bf16[16,1024]{1,0:T(8,128)(2,1)} %param.11, bf16[16,1024]{1,0:T(8,128)(2,1)} %param.10, bf16[16,4096]{1,0:T(8,128)(2,1)} %param.9), kind=kLoop, calls=%fused_computation | loop fusion | flops 589824 | bytes 393216 | tf_op jit(solution)/shard_map/concatenate | solution.py:505
  1.5 0.0 copy-done
  1.6 0.0 copy-done.1
  1.6 0.0 copy-done.2
  1.6 0.0 copy-done.3
  1.6 0.1 pad_add_fusion.head_ref.table_ref
  1.7 0.6 %shard_map.91 = bf16[8,16,768]{2,1,0:T(8,128)(2,1)S(1)} custom-call(s32[32]{0:T(128)S(1)} %pad_add_fusion.head_ref.table_ref, bf16[16,6144]{1,0:T(8,128)(2,1)S(1)} %pad_maximum_fusion.in_ref), custom_call_target="tpu_custom_call" | custom-call | tf_op jit(solution)/shard_map/pallas_call | solution.py:508
  2.2 15.2 %all_to_all.10 = bf16[8,16,768]{2,1,0:T(8,128)(2,1)S(1)} all-to-all(bf16[8,16,768]{2,1,0:T(8,128)(2,1)S(1)} %shard_map.91), channel_id=1, replica_groups=mesh['rep'=2,'head'=8,'seq'=2] {'head'}, dimensions={0} | all-to-all | bytes 393216 | tf_op jit(solution)/shard_map/all_to_all | solution.py:515
  17.5 0.0 collective-permute-start
  17.5 0.0 collective-permute-done.1.k_peer
  17.5 0.0 collective-permute-done.2.v_peer
  17.5 6.4 %shard_map.92 = (f32[128,512]{1,0:T(8,128)S(1)}, f32[16,512]{1,0:T(8,128)S(1)}) custom-call(s32[32]{0:T(128)S(1)} %pad_add_fusion.head_ref.table_ref, bf16[128,768]{1,0:T(8,128)(2,1)S(1)} %bitcast.5, bf16[4096,128]{1,0:T(8,128)(2,1)S(1)} %collective-permute-done.1.k_peer, bf16[4096,128]{1,0:T(8,128)(2,1)S(1)} %collective-permute-done.2.v_peer, ...), custom_call_target="tpu_custom_call" | custom-call | tf_op jit(solution)/shard_map/pallas_call | solution.py:521
  23.9 0.0 collective-permute-done.peer_ref
  23.9 1.1 %shard_map.93 = bf16[128,512]{1,0:T(8,128)(2,1)S(1)} custom-call(s32[32]{0:T(128)S(1)} %pad_add_fusion.head_ref.table_ref, bf16[128,768]{1,0:T(8,128)(2,1)S(1)} %bitcast.6, bf16[128,768]{1,0:T(8,128)(2,1)S(1)} %collective-permute-done.peer_ref, f32[128,512]{1,0:T(8,128)S(1)} %get-tuple-element.17.acc_ref, f32[16,512]{1,0:T(8,128)S(1)} %get-tuple-element.18.stat_ref), custom_call_target="tpu_custom_call" | custom-call | tf_op jit(solution)/shard_map/pallas_call | solution.py:544
  24.9 10.6 %all_to_all.11.in_ref = bf16[8,16,512]{2,1,0:T(8,128)(2,1)S(1)} all-to-all(bf16[8,16,512]{2,1,0:T(8,128)(2,1)S(1)} %bitcast.7), channel_id=1, replica_groups=mesh['rep'=2,'head'=8,'seq'=2] {'head'}, dimensions={0} | all-to-all | bytes 262144 | tf_op jit(solution)/shard_map/all_to_all | solution.py:558
  35.5 1.3 %shard_map.94 = bf16[16,4096]{1,0:T(8,128)(2,1)} custom-call(s32[32]{0:T(128)S(1)} %pad_add_fusion.head_ref.table_ref, bf16[8,16,512]{2,1,0:T(8,128)(2,1)S(1)} %all_to_all.11.in_ref), custom_call_target="tpu_custom_call" | custom-call | tf_op jit(solution)/shard_map/pallas_call | solution.py:559
Async XLA Ops:
  0.0 17.5 %collective-permute-start.1 = (bf16[4096,128]{1,0:T(8,128)(2,1)}, bf16[4096,128]{1,0:T(8,128)(2,1)S(1)}, u32[]{:S(2)}, u32[]{:S(2)}) collective-permute-start(bf16[4096,128]{1,0:T(8,128)(2,1)} %bitcast.8), channel_id=1, source_target_pairs={{0,1},{1,0},{2,3},{3,2},{4,5},{5,4},{6,7},{7,6},{8,9},{9,8},{10,11... | collective-permute-start | bytes 3145736 | tf_op jit(solution)/shard_map/ppermute | solution.py:503
  0.5 1.1 %copy-start = (s32[8]{0:T(128)S(1)}, s32[8]{0:T(128)}, u32[]{:S(2)}) copy-start(s32[8]{0:T(128)} %param.17) | copy-start | bytes 100
  0.5 1.1 %copy-start.1 = (s32[8]{0:T(128)S(1)}, s32[8]{0:T(128)}, u32[]{:S(2)}) copy-start(s32[8]{0:T(128)} %param.16) | copy-start | bytes 100
  0.5 1.1 %copy-start.2 = (s32[8]{0:T(128)S(1)}, s32[8]{0:T(128)}, u32[]{:S(2)}) copy-start(s32[8]{0:T(128)} %param.15) | copy-start | bytes 100
  0.5 1.1 %copy-start.3 = (s32[8]{0:T(128)S(1)}, s32[8]{0:T(128)}, u32[]{:S(2)}) copy-start(s32[8]{0:T(128)} %param.14) | copy-start | bytes 100
  0.5 17.0 %collective-permute-start.2 = (bf16[4096,128]{1,0:T(8,128)(2,1)}, bf16[4096,128]{1,0:T(8,128)(2,1)S(1)}, u32[]{:S(2)}, u32[]{:S(2)}) collective-permute-start(bf16[4096,128]{1,0:T(8,128)(2,1)} %bitcast.10), channel_id=1, source_target_pairs={{0,1},{1,0},{2,3},{3,2},{4,5},{5,4},{6,7},{7,6},{8,9},{9,8},{10,11... | collective-permute-start | bytes 3145736 | tf_op jit(solution)/shard_map/ppermute | solution.py:504
  17.5 6.4 %collective-permute-start = (bf16[128,768]{1,0:T(8,128)(2,1)S(1)}, bf16[128,768]{1,0:T(8,128)(2,1)S(1)}, u32[]{:S(2)}, u32[]{:S(2)}) collective-permute-start(bf16[128,768]{1,0:T(8,128)(2,1)S(1)} %bitcast.4), channel_id=1, source_target_pairs={{0,1},{1,0},{2,3},{3,2},{4,5},{5,4},{6,7},{7,6},{8,9},{9,8},{10,11... | collective-permute-start | bytes 589832 | tf_op jit(solution)/shard_map/ppermute | solution.py:517

commit v8 on v6

--- a/solution.py
+++ b/solution.py
@@ -515,7 +515,7 @@
     recv = lax.all_to_all(send, "head", split_axis=0, concat_axis=0, tiled=True)
     recv = recv.reshape(tokens, group_width + 2 * head_dim)
     peer = lax.ppermute(recv, "seq", swap)
-    key_block = math.gcd(ctx_dev, 1024)
+    key_block = math.gcd(ctx_dev, 512)
     row_block = 256
     keys = 2 * ctx_dev + tokens
     acc, stat = pl.pallas_call(

time: 36.5 us -> 37.8 us (1.036); the launches traced: 36.1 us -> 38.2 us
  blocking collectives: 25.8 us -> 27.9 us
    all_to_all x1, blocking collectives: 10.6 us -> 12.7 us  [on_device_pairs(): lax.all_to_all(result, 'head', split_axis=0, concat_axis=0, tiled=True)]
  transfers between devices with their start and end apart: 3 -> 3, of which waited for: 0 -> 0; matrix products, arithmetic and copies ran while one was open for 3% -> 3% of each run, Pallas kernels for 17% -> 16%
where the time goes in v8:
time: 37.8 us; the launch traced here: 38.2 us
  blocking collectives  27.9 us (74%)
  Pallas kernels  8.59 us (23%)
  other arithmetic  1.04 us (3%)
  starting transfers between devices  0.58 us (2%)
    all_to_all x1, blocking collectives, on_device_pairs(): recv = lax.all_to_all(send, 'head', split_axis=0, concat_axis=0, tiled=True)  15.2 us
    all_to_all x1, blocking collectives, on_device_pairs(): lax.all_to_all(result, 'head', split_axis=0, concat_axis=0, tiled=True)  12.7 us
    pallas_call x1, Pallas kernels, on_device_pairs(): pl.pallas_call(functools.partial(attend_kernel, tok_rows=tok_rows, group_...  5.7 us
    pallas_call x1, Pallas kernels, on_device_pairs(): pl.pallas_call(unpack_kernel, out_shape=jax.ShapeDtypeStruct((tok_rows, K...  1.26 us
    pallas_call x1, Pallas kernels, on_device_pairs(): pl.pallas_call(functools.partial(span_kernel, tok_rows=tok_rows, group_he...  1.07 us
    concatenate x1, other arithmetic, on_device_pairs(): joined = jnp.concatenate([q_span, k_span, v_span], axis=1)  0.96 us
  transfers between devices with their start and end apart: 3, of which 0 were waited for; matrix products, arithmetic and copies ran while one was open for 3% of the time, Pallas kernels for 16%

profile of v8, /device:TPU:0, one launch (start us, length us, event | category | flops | bytes accessed | tf_op | source)
XLA Modules:
  0.0 38.2 jit_solution(5945102731615685360)
XLA Ops:
  0.0 0.5 %collective-permute-start.1 = (bf16[4096,128]{1,0:T(8,128)(2,1)}, bf16[4096,128]{1,0:T(8,128)(2,1)S(1)}, u32[]{:S(2)}, u32[]{:S(2)}) collective-permute-start(bf16[4096,128]{1,0:T(8,128)(2,1)} %bitcast.8), channel_id=1, source_target_pairs={{0,1},{1,0},{2,3},{3,2},{4,5},{5,4},{6,7},{7,6},{8,9},{9,8},{10,11... | collective-permute-start | bytes 3145736 | tf_op jit(solution)/shard_map/ppermute | solution.py:503
  0.5 0.0 copy-start
  0.5 0.0 copy-start.1
  0.5 0.0 copy-start.2
  0.5 0.0 copy-start.3
  0.5 0.1 collective-permute-start.2
  0.6 1.0 %pad_maximum_fusion.in_ref = bf16[16,6144]{1,0:T(8,128)(2,1)S(1)} fusion(bf16[16,1024]{1,0:T(8,128)(2,1)} %param.11, bf16[16,1024]{1,0:T(8,128)(2,1)} %param.10, bf16[16,4096]{1,0:T(8,128)(2,1)} %param.9), kind=kLoop, calls=%fused_computation | loop fusion | flops 589824 | bytes 393216 | tf_op jit(solution)/shard_map/concatenate | solution.py:505
  1.5 0.0 copy-done
  1.6 0.0 copy-done.1
  1.6 0.0 copy-done.2
  1.6 0.0 copy-done.3
  1.6 0.1 pad_add_fusion.head_ref.table_ref
  1.7 0.6 %shard_map.91 = bf16[8,16,768]{2,1,0:T(8,128)(2,1)S(1)} custom-call(s32[32]{0:T(128)S(1)} %pad_add_fusion.head_ref.table_ref, bf16[16,6144]{1,0:T(8,128)(2,1)S(1)} %pad_maximum_fusion.in_ref), custom_call_target="tpu_custom_call" | custom-call | tf_op jit(solution)/shard_map/pallas_call | solution.py:508
  2.2 15.2 %all_to_all.10 = bf16[8,16,768]{2,1,0:T(8,128)(2,1)S(1)} all-to-all(bf16[8,16,768]{2,1,0:T(8,128)(2,1)S(1)} %shard_map.91), channel_id=1, replica_groups=mesh['rep'=2,'head'=8,'seq'=2] {'head'}, dimensions={0} | all-to-all | bytes 393216 | tf_op jit(solution)/shard_map/all_to_all | solution.py:515
  17.5 0.0 collective-permute-start
  17.5 0.0 collective-permute-done.1.k_peer
  17.5 0.0 collective-permute-done.2.v_peer
  17.5 5.7 %shard_map.92 = (f32[128,512]{1,0:T(8,128)S(1)}, f32[16,512]{1,0:T(8,128)S(1)}) custom-call(s32[32]{0:T(128)S(1)} %pad_add_fusion.head_ref.table_ref, bf16[128,768]{1,0:T(8,128)(2,1)S(1)} %bitcast.5, bf16[4096,128]{1,0:T(8,128)(2,1)S(1)} %collective-permute-done.1.k_peer, bf16[4096,128]{1,0:T(8,128)(2,1)S(1)} %collective-permute-done.2.v_peer, ...), custom_call_target="tpu_custom_call" | custom-call | tf_op jit(solution)/shard_map/pallas_call | solution.py:521
  23.2 0.0 collective-permute-done.peer_ref
  23.2 1.1 %shard_map.93 = bf16[128,512]{1,0:T(8,128)(2,1)S(1)} custom-call(s32[32]{0:T(128)S(1)} %pad_add_fusion.head_ref.table_ref, bf16[128,768]{1,0:T(8,128)(2,1)S(1)} %bitcast.6, bf16[128,768]{1,0:T(8,128)(2,1)S(1)} %collective-permute-done.peer_ref, f32[128,512]{1,0:T(8,128)S(1)} %get-tuple-element.17.acc_ref, f32[16,512]{1,0:T(8,128)S(1)} %get-tuple-element.18.stat_ref), custom_call_target="tpu_custom_call" | custom-call | tf_op jit(solution)/shard_map/pallas_call | solution.py:544
  24.3 12.7 %all_to_all.11.in_ref = bf16[8,16,512]{2,1,0:T(8,128)(2,1)S(1)} all-to-all(bf16[8,16,512]{2,1,0:T(8,128)(2,1)S(1)} %bitcast.7), channel_id=1, replica_groups=mesh['rep'=2,'head'=8,'seq'=2] {'head'}, dimensions={0} | all-to-all | bytes 262144 | tf_op jit(solution)/shard_map/all_to_all | solution.py:558
  36.9 1.3 %shard_map.94 = bf16[16,4096]{1,0:T(8,128)(2,1)} custom-call(s32[32]{0:T(128)S(1)} %pad_add_fusion.head_ref.table_ref, bf16[8,16,512]{2,1,0:T(8,128)(2,1)S(1)} %all_to_all.11.in_ref), custom_call_target="tpu_custom_call" | custom-call | tf_op jit(solution)/shard_map/pallas_call | solution.py:559
Async XLA Ops:
  0.0 17.5 %collective-permute-start.1 = (bf16[4096,128]{1,0:T(8,128)(2,1)}, bf16[4096,128]{1,0:T(8,128)(2,1)S(1)}, u32[]{:S(2)}, u32[]{:S(2)}) collective-permute-start(bf16[4096,128]{1,0:T(8,128)(2,1)} %bitcast.8), channel_id=1, source_target_pairs={{0,1},{1,0},{2,3},{3,2},{4,5},{5,4},{6,7},{7,6},{8,9},{9,8},{10,11... | collective-permute-start | bytes 3145736 | tf_op jit(solution)/shard_map/ppermute | solution.py:503
  0.5 1.1 %copy-start = (s32[8]{0:T(128)S(1)}, s32[8]{0:T(128)}, u32[]{:S(2)}) copy-start(s32[8]{0:T(128)} %param.17) | copy-start | bytes 100
  0.5 1.1 %copy-start.1 = (s32[8]{0:T(128)S(1)}, s32[8]{0:T(128)}, u32[]{:S(2)}) copy-start(s32[8]{0:T(128)} %param.16) | copy-start | bytes 100
  0.5 1.1 %copy-start.2 = (s32[8]{0:T(128)S(1)}, s32[8]{0:T(128)}, u32[]{:S(2)}) copy-start(s32[8]{0:T(128)} %param.15) | copy-start | bytes 100
  0.5 1.1 %copy-start.3 = (s32[8]{0:T(128)S(1)}, s32[8]{0:T(128)}, u32[]{:S(2)}) copy-start(s32[8]{0:T(128)} %param.14) | copy-start | bytes 100
  0.5 17.0 %collective-permute-start.2 = (bf16[4096,128]{1,0:T(8,128)(2,1)}, bf16[4096,128]{1,0:T(8,128)(2,1)S(1)}, u32[]{:S(2)}, u32[]{:S(2)}) collective-permute-start(bf16[4096,128]{1,0:T(8,128)(2,1)} %bitcast.10), channel_id=1, source_target_pairs={{0,1},{1,0},{2,3},{3,2},{4,5},{5,4},{6,7},{7,6},{8,9},{9,8},{10,11... | collective-permute-start | bytes 3145736 | tf_op jit(solution)/shard_map/ppermute | solution.py:504
  17.5 5.7 %collective-permute-start = (bf16[128,768]{1,0:T(8,128)(2,1)S(1)}, bf16[128,768]{1,0:T(8,128)(2,1)S(1)}, u32[]{:S(2)}, u32[]{:S(2)}) collective-permute-start(bf16[128,768]{1,0:T(8,128)(2,1)S(1)} %bitcast.4), channel_id=1, source_target_pairs={{0,1},{1,0},{2,3},{3,2},{4,5},{5,4},{6,7},{7,6},{8,9},{9,8},{10,11... | collective-permute-start | bytes 589832 | tf_op jit(solution)/shard_map/ppermute | solution.py:517
